TPU v7x, 32 devices: a whole 2x2x4 slice. The times are simulated.
32 devices in a mesh: grp: 8 (over z, core), dev: 4 (over y, x).
Axes of the slice: x: 2, y: 2, z: 4, core: 2. Of those that a mesh axis runs over, the one named last changes fastest.
Arguments:
- voxel_features: float32 [128, 64, 512], P(('grp', 'dev')), may hold values from -6 to 6
- fine_links: int32 [128, 26], P(('grp', 'dev')), may hold values from -1 to 127, as said below
- parent_codes: int32 [128], P(('grp', 'dev')), may hold values from 0 to 63, as said below
- coarse_links: int32 [64, 26], P(('grp', 'dev')), may hold values from -1 to 63, as said below
- fine_in_weight: float32 [64, 1728], replicated, may hold values from -0.15625 to 0.15625
- fine_in_bias: float32 [64], replicated, may hold values from -3 to 3
- down_weight: float32 [128, 64], replicated, may hold values from -0.75 to 0.75
- coarse_first_weight: float32 [128, 3456], replicated, may hold values from -0.109375 to 0.109375
- coarse_first_bias: float32 [128], replicated, may hold values from -3 to 3
- coarse_second_weight: float32 [128, 3456], replicated, may hold values from -0.109375 to 0.109375
- coarse_second_bias: float32 [128], replicated, may hold values from -3 to 3
- up_weight: float32 [64, 128], replicated, may hold values from -0.5 to 0.5
- fine_out_weight: float32 [64, 1728], replicated, may hold values from -0.15625 to 0.15625
- fine_out_bias: float32 [64], replicated, may hold values from -3 to 3
Outputs:
- refined: float32 [128, 64, 512], P(('grp', 'dev'))
Inputs may be any that keep to these rules, and one draw needn't show every extreme that they name: `fine_links`: devices are numbered along grp then dev, device d holding bricks d * 4 to (d + 1) * 4 - 1. An entry is -1 or a brick from d * 4 - 2 to (d + 1) * 4 + 1 for a brick of device d, with 2 = 2. parent_codes[i] = 8 * 2 * owner + 8 * slot + octant: owner is the dev index, within the brick's group of 4 devices, of the device that holds the parent, slot the parent's slot there (0 to 1), and octant = 4 * a + 2 * b + c the child's octant. Within a group all codes differ; the number of slots in use differs from device to device, and some device of every group uses all 2. `coarse_links`: device d holds slots d * 2 to (d + 1) * 2 - 1. An entry is -1 or a slot from (d - 1) * 2 to (d + 2) * 2 - 1 for a slot of device d.
All inputs are finite; a program needn't handle non-finite values.
Results may differ from a plain program's by a relative error of at most 0.0001.
Values sent between devices are 32-bit elements; how exact they have to be, the bound alone decides.
A program may use at most 128 MiB of HBM per device.

v0:
```python
import functools

import jax
import jax.numpy as jnp
from jax import lax
from jax.experimental import pallas as pl
from jax.experimental.pallas import tpu as pltpu
from jax.sharding import PartitionSpec as P

F32 = jnp.float32
BF16 = jnp.bfloat16
MESH = pl.DeviceIdType.MESH
SIDE = 8
VOX = SIDE * SIDE * SIDE
OCT = VOX // 8
PADDED = SIDE + 2
HALO = 2
FINE_ROWS = 304
COARSE_ROWS = 296
LIMIT = 60 * 1024 * 1024

offsets = [(x, y, z) for x in (-1, 0, 1) for y in (-1, 0, 1) for z in (-1, 0, 1)]
columns = {o: k for k, o in enumerate(o for o in offsets if o != (0, 0, 0))}
source = {-1: slice(7, 8), 0: slice(0, 8), 1: slice(0, 1)}
target = {-1: slice(0, 1), 0: slice(1, 9), 1: slice(9, 10)}


def split(v):
    high = v.astype(BF16).astype(F32)
    return high, v - high


def silu(v):
    return v / (1.0 + jnp.exp(-v))


def product(a, b, dims=((1,), (1,))):
    return lax.dot_general(a, b, (dims, ((), ())), preferred_element_type=F32)


def precise(a, b, dims=((1,), (1,))):
    (a_high, a_low), (b_high, b_low) = split(a), split(b)
    a_high, a_low, b_high, b_low = (v.astype(BF16) for v in (a_high, a_low, b_high, b_low))
    return product(a_high, b_high, dims) + product(a_low, b_high, dims) + product(a_high, b_low, dims)


def spread(v):
    half = v.shape[0] // 2
    return jnp.concatenate([v[:half], v[half:]], axis=1)


def unspread(v):
    width = v.shape[1] // 2
    return jnp.concatenate([v[:, :width], v[:, width:]], axis=0)


def surface_rank(p):
    x, y, z = p // 64, p // 8 % 8, p % 8
    inner = jnp.where(z == 0, 0, jnp.where(z == 7, 1, -1))
    inner = jnp.where(inner < 0, -1, 224 + ((x - 1) * 6 + y - 1) * 2 + inner)
    side = 128 + (x - 1) * 16 + z
    edge = jnp.where(y == 0, side, jnp.where(y == 7, side + 8, inner))
    return jnp.where(x == 0, p, jnp.where(x == 7, p - 384, edge))


def surface_pick(rows):
    rank = surface_rank(lax.broadcasted_iota(jnp.int32, (1, VOX), 1))
    row = lax.broadcasted_iota(jnp.int32, (rows, VOX), 0)
    return jnp.where(row == rank, 1.0, 0.0).astype(BF16)


def surface_place(rows):
    rank = surface_rank(lax.broadcasted_iota(jnp.int32, (VOX, rows), 0))
    col = lax.broadcasted_iota(jnp.int32, (VOX, rows), 1)
    return jnp.where(col == rank, 1.0, 0.0).astype(BF16)


def both_parts(v):
    high, low = split(v)
    return jnp.concatenate([high, low], axis=1).astype(BF16)


def joined(sums):
    width = sums.shape[1] // 2
    return sums[:, :width] + sums[:, width:]


def put_surface(parts, index, placing, v):
    sums = product(placing, both_parts(v), ((1,), (0,)))
    parts[index] = sums.reshape(SIDE, SIDE, SIDE, sums.shape[1])


def put_parts(parts, index, v):
    high, low = split(v)
    parts[index] = jnp.concatenate([high, low], axis=1).reshape(SIDE, SIDE, SIDE, 2 * v.shape[1])


def fill(parts, own, start, links, brick, padded):
    for dx, dy, dz in offsets:
        spot = (dz + 1, target[dx], target[dy])
        if (dx, dy, dz) == (0, 0, 0):
            padded[spot] = parts[own]
            continue
        link = links[brick, columns[dx, dy, dz]]
        found = link >= 0
        row = jnp.where(found, link - start, own)
        keep = jnp.where(found, 1.0, 0.0).astype(F32)
        padded[spot] = parts[row, source[dx], source[dy]] * keep


def unfold(padded, patches):
    width = padded.shape[-1]
    z_at = lax.broadcasted_iota(jnp.int32, (PADDED, SIDE, width), 1)
    for x in range(PADDED):
        middle = padded[1, x]
        padded[0, x] = pltpu.roll(jnp.where(z_at == SIDE - 1, padded[0, x], middle), 1, 1)
        padded[2, x] = pltpu.roll(jnp.where(z_at == 0, padded[2, x], middle), SIDE - 1, 1)
    for i in range(3):
        for j in range(3):
            for k in range(3):
                tap = 9 * i + 3 * j + k
                window = padded[k, i : i + SIDE, j : j + SIDE].reshape(VOX, width)
                patches[:, tap * width : (tap + 1) * width] = window.astype(BF16)


def fine_matrix(weight, matrix):
    channels = weight.shape[0]
    lane = lax.broadcasted_iota(jnp.int32, (channels, 2 * channels), 1)
    for pair in range(14):
        if pair < 13:
            tile = weight[:, pair * 2 * channels : (pair + 1) * 2 * channels]
            turned = pltpu.roll(tile, channels, 1)
            taps = [
                jnp.where(lane < channels, tile, turned),
                jnp.where(lane < channels, turned, tile),
            ]
        else:
            tile = weight[:, 26 * channels : 27 * channels]
            taps = [jnp.concatenate([tile, tile], axis=1)]
        for at, tap in enumerate(taps):
            high, low = split(tap)
            cols = slice((2 * pair + at) * 2 * channels, (2 * pair + at + 1) * 2 * channels)
            matrix[0:channels, cols] = high.astype(BF16)
            matrix[channels : 2 * channels, cols] = low.astype(BF16)


def coarse_matrix(weight, matrix):
    channels = weight.shape[0]
    for tap in range(27):
        high, low = split(weight[:, tap * channels : (tap + 1) * channels])
        for part in range(2):
            cols = slice((2 * tap + part) * channels, (2 * tap + part + 1) * channels)
            matrix[0:channels, cols] = high.astype(BF16)
            matrix[channels : 2 * channels, cols] = low.astype(BF16)


def convolved(parts, own, start, links, brick, padded, patches, matrix, bias):
    fill(parts, own, start, links, brick, padded)
    unfold(padded, patches)
    both = product(patches[...], matrix[...])
    channels = both.shape[1] // 2
    return both[:, :channels] + both[:, channels:] + bias[...]


def place():
    return lax.axis_index("grp"), lax.axis_index("dev"), lax.axis_size("grp"), lax.axis_size("dev")


def pack_kernel(x, packed):
    pick = surface_pick(FINE_ROWS)
    for i in range(x.shape[0]):
        high, low = split(x[i])
        packed[i] = spread(product(pick, high.astype(BF16)) + product(pick, low.astype(BF16)))


def first_kernel(x, left, right, links, weight, bias, hidden, packed, pooled, parts, padded, patches, matrix):
    group, member, _, members = place()
    count = x.shape[0]
    start = (group * members + member) * count - HALO
    for i in range(count):
        put_parts(parts, HALO + i, x[i].T)
    placing = surface_place(FINE_ROWS)
    for i in range(HALO):
        put_surface(parts, i, placing, unspread(left[i]))
        put_surface(parts, HALO + count + i, placing, unspread(right[i]))
    pick = surface_pick(FINE_ROWS)
    fine_matrix(weight, matrix)
    row = lax.broadcasted_iota(jnp.int32, (OCT, VOX), 0)
    col = lax.broadcasted_iota(jnp.int32, (OCT, VOX), 1)
    cell = (col // 128) * 16 + (col // 16 % 4) * 4 + col // 2 % 4
    pooling = jnp.where(row == cell, 0.125, 0.0).astype(BF16)

    def step(i, carry):
        out = silu(
            convolved(parts, HALO + i, start, links, i, padded, patches, matrix, bias)
        )
        hidden[i] = spread(out)
        both = both_parts(out)
        pooled[i] = spread(joined(product(pooling, both, ((1,), (0,)))))
        packed[i] = spread(joined(product(pick, both, ((1,), (0,)))))
        return carry

    lax.fori_loop(0, count, step, 0)


def octant_order(flip):
    row = lax.broadcasted_iota(jnp.int32, (VOX, VOX), 1 if flip else 0)
    col = lax.broadcasted_iota(jnp.int32, (VOX, VOX), 0 if flip else 1)
    x, y, z = row // 64, row // 8 % 8, row % 8
    spot = (x // 4 * 4 + y // 4 * 2 + z // 4) * 64 + x % 4 * 16 + y % 4 * 4 + z % 4
    return jnp.where(spot == col, 1.0, 0.0).astype(BF16)


def second_kernel(pooled, codes, links, down, weight, bias, first, packed, pieces, parts, padded, patches, matrix):
    group, member, groups, members = place()
    slots = links.shape[0]
    count = pooled.shape[1]
    start = (group * members + member - 1) * slots
    position = group * members + member
    pieces[...] = jnp.zeros_like(pieces)
    coarse_matrix(weight, matrix)
    for near in range(3):
        there = position + near - 1
        there_group = (there + members) // members - 1
        there_member = there - there_group * members
        band = there_group - group + 1
        valid = (there >= 0) & (there < groups * members)
        for one in range(count):

            def visit(owner, carry):
                code = codes[(band * members + owner) * 8, one] - there_member * slots * 8

                @pl.when(valid & (code >= 0) & (code < slots * 8))
                def _():
                    pieces[near * slots * 8 + code] = unspread(
                        pooled[band * members + owner, one]
                    )

                return carry

            lax.fori_loop(0, members, visit, 0)
    order = octant_order(False)

    def base(slot, carry):
        piece = pieces[pl.ds(slot * 8, 8)].reshape(VOX, pieces.shape[-1])
        lifted = precise(piece, down[...], ((1,), (0,)))
        high, low = split(lifted)
        both = jnp.concatenate([high, low], axis=1).astype(BF16)
        parts[slot] = product(order, both, ((1,), (0,))).reshape(SIDE, SIDE, SIDE, both.shape[1])
        return carry

    lax.fori_loop(0, 3 * slots, base, 0)
    pick = surface_pick(COARSE_ROWS)

    def step(i, carry):
        out = silu(
            convolved(parts, slots + i, start, links, i, padded, patches, matrix, bias)
        )
        first[i] = out
        packed[i] = joined(product(pick, both_parts(out), ((1,), (0,))))
        return carry

    lax.fori_loop(0, slots, step, 0)


def third_kernel(first, left, right, links, codes, weight, bias, up, wanted, lifted, parts, padded, patches, matrix):
    group, member, _, members = place()
    slots = links.shape[0]
    start = (group * members + member - 1) * slots
    coarse_matrix(weight, matrix)
    placing = surface_place(COARSE_ROWS)
    for i in range(slots):
        put_surface(parts, i, placing, left[i])
        put_parts(parts, slots + i, first[i])
        put_surface(parts, 2 * slots + i, placing, right[i])
    order = octant_order(True)

    def step(i, carry):
        out = silu(
            convolved(parts, slots + i, start, links, i, padded, patches, matrix, bias)
        )
        high, low = split(precise(out, up[...]))
        both = jnp.concatenate([high, low], axis=1).astype(BF16)
        sums = product(order, both, ((1,), (0,)))
        width = high.shape[1]
        ordered = sums[:, :width] + sums[:, width:]
        for octant in range(8):
            lifted[i * 8 + octant] = spread(ordered[octant * OCT : (octant + 1) * OCT])
        return carry

    lax.fori_loop(0, slots, step, 0)
    bricks = wanted.shape[0] - 2 * HALO
    each = bricks // members
    zeros = jnp.zeros((HALO,) + wanted.shape[1:], F32)
    wanted[0:HALO] = zeros
    wanted[HALO + bricks :] = zeros

    def choose(j, carry):
        code = codes[(members + j // each) * 8, j % each] - member * slots * 8
        mine = (code >= 0) & (code < slots * 8)
        keep = jnp.where(mine, 1.0, 0.0).astype(F32)
        wanted[HALO + j] = lifted[jnp.where(mine, code, 0)] * keep
        return carry

    lax.fori_loop(0, bricks, choose, 0)


def fourth_kernel(x, hidden, left, right, window, low, high, links, weight, bias, out, parts, padded, patches, matrix):
    group, member, groups, members = place()
    count = x.shape[0]
    start = (group * members + member) * count - HALO
    fine_matrix(weight, matrix)
    row = lax.broadcasted_iota(jnp.int32, (VOX, OCT), 0)
    col = lax.broadcasted_iota(jnp.int32, (VOX, OCT), 1)
    cell = (row // 128) * 16 + (row // 16 % 4) * 4 + row // 2 % 4
    repeat = jnp.where(col == cell, 1.0, 0.0).astype(BF16)
    placing = surface_place(FINE_ROWS)
    for i in range(count + 2 * HALO):
        piece = window[0, i]
        for owner in range(1, members):
            piece = piece + window[owner, i]
        if i < HALO:
            other = low[0, i]
            for owner in range(1, members):
                other = other + low[owner, i]
            piece = jnp.where(member == 0, other, piece)
        elif i >= HALO + count:
            other = high[0, i - HALO - count]
            for owner in range(1, members):
                other = other + high[owner, i - HALO - count]
            piece = jnp.where(member == members - 1, other, piece)
        rising = joined(product(repeat, both_parts(unspread(piece)), ((1,), (0,))))
        if i < HALO:
            held = joined(
                product(placing, both_parts(unspread(left[i])), ((1,), (0,)))
            )
        elif i < HALO + count:
            held = unspread(hidden[i - HALO])
        else:
            held = joined(
                product(placing, both_parts(unspread(right[i - HALO - count])), ((1,), (0,)))
            )
        put_parts(parts, i, silu(held + rising))

    def step(i, carry):
        conv = convolved(parts, HALO + i, start, links, i, padded, patches, matrix, bias)
        out[i] = x[i] + conv.T
        return carry

    lax.fori_loop(0, count, step, 0)


def exchange_kernel(margins, shared, windows, *refs):
    halos = len(margins)
    total = halos + shared + windows
    given = 2 * halos + shared + 3 * windows
    ins, outs = refs[:total], refs[total : total + given]
    send_halo, recv_halo, send_all, recv_all = refs[total + given :]
    group, member, groups, members = place()
    position = group * members + member
    whole = groups * members
    has_left, has_right = position > 0, position < whole - 1
    has_low, has_high = group > 0, group < groups - 1
    left_at = (jnp.maximum(position - 1, 0) // members, (position + members - 1) % members)
    right_at = (jnp.minimum(position + 1, whole - 1) // members, (position + 1) % members)
    low_at = (jnp.maximum(group - 1, 0), members - 1)
    high_at = (jnp.minimum(group + 1, groups - 1), 0)

    barrier = pltpu.get_barrier_semaphore()

    def greet(where):
        pl.semaphore_signal(barrier, inc=1, device_id=where, device_id_type=MESH)

    count = jnp.int32(0)
    if halos:
        pl.when(has_left)(lambda: greet(left_at))
        pl.when(has_right)(lambda: greet(right_at))
        count = count + jnp.where(has_left, 1, 0) + jnp.where(has_right, 1, 0)
    if shared or windows:
        for k in range(1, members):
            greet((group, (member + k) % members))
        for k in range(members):
            pl.when((member == 0) & has_low)(lambda k=k: greet((low_at[0], k)))
            pl.when((member == members - 1) & has_high)(lambda k=k: greet((high_at[0], k)))
        count = count + (members - 1) + jnp.where(has_low, 1, 0) + jnp.where(has_high, 1, 0)
    pl.semaphore_wait(barrier, count)

    def remote(src, dst, send, recv, where):
        return pltpu.make_async_remote_copy(
            src_ref=src, dst_ref=dst, send_sem=send, recv_sem=recv,
            device_id=where, device_id_type=MESH,
        )

    def parts_of(a):
        src = ins[halos + a]
        if a < shared:
            out = outs[2 * halos + a]
            return (
                lambda to: src, src, src,
                lambda by: out.at[members + by],
                lambda by: out.at[by],
                lambda by: out.at[2 * members + by],
            )
        window, low, high = outs[2 * halos + shared + 3 * (a - shared) :][:3]
        span = window.shape[1]
        each = span - 2 * HALO
        bricks = src.shape[0] - 2 * HALO
        return (
            lambda to: src.at[pl.ds(to * each, span)],
            src.at[bricks : bricks + HALO],
            src.at[HALO : 2 * HALO],
            lambda by: window.at[by],
            lambda by: low.at[by],
            lambda by: high.at[by],
        )

    def each(action):
        for a in range(shared + windows):
            own, up, down, here, below, above = parts_of(a)
            sends, recvs = send_all.at[a], recv_all.at[a]
            for k in range(1, members):
                other = (member + k) % members
                by = member if action == "start" else other
                copy = remote(
                    own(other), here(by), sends.at[k], recvs.at[members + by], (group, other)
                )
                copy.start() if action == "start" else copy.wait()
            to_high = remote(up, below(member), sends.at[0], recvs.at[member], high_at)
            to_low = remote(
                down, above(member), sends.at[members], recvs.at[2 * members + member], low_at
            )
            if action == "start":
                pl.when(has_high)(to_high.start)
                pl.when(has_low)(to_low.start)
            else:
                pl.when(has_high)(to_high.wait_send)
                pl.when(has_low)(to_low.wait_send)
                for k in range(members):
                    from_low = remote(up, below(k), sends.at[0], recvs.at[k], low_at)
                    from_high = remote(
                        down, above(k), sends.at[0], recvs.at[2 * members + k], high_at
                    )
                    pl.when((member == 0) & has_low)(from_low.wait_recv)
                    pl.when((member == members - 1) & has_high)(from_high.wait_recv)
        for a, margin in enumerate(margins):
            src, before, after = ins[a], outs[2 * a], outs[2 * a + 1]
            length = src.shape[0]
            to_right = remote(
                src.at[length - margin : length], before, send_halo.at[a, 0],
                recv_halo.at[a, 0], right_at,
            )
            to_left = remote(
                src.at[0:margin], after, send_halo.at[a, 1], recv_halo.at[a, 1], left_at
            )
            if action == "start":
                pl.when(has_right)(to_right.start)
                pl.when(has_left)(to_left.start)
            else:
                pl.when(has_right)(to_right.wait_send)
                pl.when(has_left)(to_left.wait_send)
                pl.when(has_left)(to_right.wait_recv)
                pl.when(has_right)(to_left.wait_recv)

    each("start")
    for a in range(shared):
        outs[2 * halos + a][members + member] = ins[halos + a][...]
    for a in range(shared, shared + windows):
        window, src = outs[2 * halos + shared + 3 * (a - shared)], ins[halos + a]
        span = window.shape[1]
        window[member] = src[pl.ds(member * (span - 2 * HALO), span)]
    each("wait")


def exchange(halos, shared, windows, number):
    members = lax.axis_size("dev")
    shapes = []
    for array, margin in halos:
        shapes += [jax.ShapeDtypeStruct((margin,) + array.shape[1:], array.dtype)] * 2
    for array in shared:
        shapes.append(jax.ShapeDtypeStruct((3 * members,) + array.shape, array.dtype))
    for array in windows:
        span = (array.shape[0] - 2 * HALO) // members + 2 * HALO
        for rows in (span, HALO, HALO):
            shapes.append(
                jax.ShapeDtypeStruct((members, rows) + array.shape[1:], array.dtype)
            )
    total = len(halos) + len(shared) + len(windows)
    vmem = pl.BlockSpec(memory_space=pltpu.VMEM)
    halo_count, share_count = max(len(halos), 1), max(len(shared) + len(windows), 1)
    return pl.pallas_call(
        functools.partial(exchange_kernel, [m for _, m in halos], len(shared), len(windows)),
        out_shape=shapes,
        in_specs=[vmem] * total,
        out_specs=[vmem] * len(shapes),
        scratch_shapes=[
            pltpu.SemaphoreType.DMA((halo_count, 2)),
            pltpu.SemaphoreType.DMA((halo_count, 2)),
            pltpu.SemaphoreType.DMA((share_count, members + 1)),
            pltpu.SemaphoreType.DMA((share_count, 3 * members)),
        ],
        name=f"exchange_{number}",
        compiler_params=pltpu.CompilerParams(
            collective_id=number, has_side_effects=True, vmem_limit_bytes=LIMIT
        ),
    )(*[a for a, _ in halos], *shared, *windows)


def local(kernel, shapes, args, scalars, scratch):
    vmem = pl.BlockSpec(memory_space=pltpu.VMEM)
    smem = pl.BlockSpec(memory_space=pltpu.SMEM)
    return pl.pallas_call(
        kernel,
        out_shape=shapes,
        in_specs=[smem if i in scalars else vmem for i in range(len(args))],
        out_specs=[vmem] * len(shapes),
        scratch_shapes=scratch,
        name=kernel.__name__,
        compiler_params=pltpu.CompilerParams(vmem_limit_bytes=LIMIT),
    )(*args)


def conv_scratch(bricks, channels):
    width = 2 * channels
    return [
        pltpu.VMEM((bricks, SIDE, SIDE, SIDE, width), F32),
        pltpu.VMEM((3, PADDED, PADDED, SIDE, width), F32),
        pltpu.VMEM((VOX, 27 * width), BF16),
        pltpu.VMEM((width, 27 * width), BF16),
    ]


def per_device(
    x, fine_links, parent_codes, coarse_links,
    in_weight, in_bias, down, one_weight, one_bias, two_weight, two_bias, up, out_weight, out_bias,
):
    count, channels = x.shape[0], x.shape[1]
    slots, wide = coarse_links.shape[0], one_bias.shape[0]
    sized = lambda *shape: jax.ShapeDtypeStruct(shape, F32)
    row = lambda bias: bias.reshape(1, -1)
    code_block = jnp.pad(parent_codes.reshape(1, -1), ((0, 7), (0, 128 - count)))
    members = lax.axis_size("dev")
    flat = (FINE_ROWS // 2, 2 * channels)
    (packed,) = local(pack_kernel, [sized(count, *flat)], [x], (), [])
    left, right, codes = exchange([(packed, HALO)], [code_block], [], 1)
    codes = codes.reshape(-1, 128)
    hidden, packed, pooled = local(
        first_kernel,
        [
            sized(count, VOX // 2, 2 * channels),
            sized(count, *flat),
            sized(count, OCT // 2, 2 * channels),
        ],
        [x, left, right, fine_links, in_weight, row(in_bias)],
        (3,),
        conv_scratch(count + 2 * HALO, channels),
    )
    hidden_left, hidden_right, pooled = exchange([(packed, HALO)], [pooled], [], 2)
    first, packed = local(
        second_kernel,
        [sized(slots, VOX, wide), sized(slots, COARSE_ROWS, wide)],
        [pooled, codes, coarse_links, down.T, one_weight, row(one_bias)],
        (1, 2),
        [pltpu.VMEM((3 * slots * 8, OCT, channels), F32)] + conv_scratch(3 * slots, wide),
    )
    first_left, first_right = exchange([(packed, slots)], [], [], 3)
    (wanted,) = local(
        third_kernel,
        [sized(members * count + 2 * HALO, OCT // 2, 2 * channels)],
        [first, first_left, first_right, coarse_links, codes, two_weight, row(two_bias), up],
        (3, 4),
        [pltpu.VMEM((slots * 8, OCT // 2, 2 * channels), F32)] + conv_scratch(3 * slots, wide),
    )
    window, low, high = exchange([], [], [wanted], 4)
    (out,) = local(
        fourth_kernel,
        [sized(count, channels, VOX)],
        [x, hidden, hidden_left, hidden_right, window, low, high, fine_links, out_weight,
         row(out_bias)],
        (7,),
        conv_scratch(count + 2 * HALO, channels),
    )
    return out


def solution(mesh):
    bricks = P(("grp", "dev"), None, None)
    rows = P(("grp", "dev"), None)
    placed = (bricks, rows, P(("grp", "dev")), rows) + (P(),) * 10
    return jax.shard_map(
        per_device, mesh=mesh, in_specs=placed, out_specs=bricks, check_vma=False
    )
```

profile of v0, /device:TPU:0, one launch (start us, length us, event | category | flops | bytes accessed | tf_op | source)
XLA Modules:
  0.0 112.8 jit_solution(14568449046511902275)
XLA Ops:
  0.0 1.3 %pad.4.refs_1_ = s32[8,128]{1,0:T(8,128)} pad(s32[1,4]{1,0:T(1,128)} %bitcast.12, s32[]{:T(128)} %constant.0.clone.1), padding=0_7x0_124 | pad | bytes 4116 | tf_op jit(solution)/shard_map/jit(_pad)/pad | solution.py:540
  1.3 2.6 %pack_kernel.1.refs_0_ = f32[4,152,128]{2,1,0:T(8,128)} custom-call(f32[4,64,512]{2,1,0:T(8,128)} %x.7), custom_call_target="tpu_custom_call" | custom-call | tf_op jit(solution)/shard_map/pack_kernel/pallas_call | solution.py:511
  3.9 14.2 %exchange_1.1 = (f32[2,152,128]{2,1,0:T(8,128)}, f32[2,152,128]{2,1,0:T(8,128)}, s32[12,8,128]{2,1,0:T(8,128)}) custom-call(f32[4,152,128]{2,1,0:T(8,128)} %pack_kernel.1.refs_0_, s32[8,128]{1,0:T(8,128)} %pad.4.refs_1_), custom_call_target="tpu_custom_call" | custom-call | tf_op jit(solution)/shard_map/exchange_1/pallas_call | solution.py:490
  18.1 11.6 %first_kernel.1 = (f32[4,256,128]{2,1,0:T(8,128)}, f32[4,152,128]{2,1,0:T(8,128)}, f32[4,32,128]{2,1,0:T(8,128)}) custom-call(f32[4,64,512]{2,1,0:T(8,128)} %x.7, f32[2,152,128]{2,1,0:T(8,128)} %get-tuple-element.21.left, f32[2,152,128]{2,1,0:T(8,128)} %get-tuple-element.22.right, s32[4,26]{1,0:T(4,128)} %links.7, f32[64,1728]{1,0:T(8,128)} %weight.4, ...), custom_call_target="tpu_custom_call" | custom-call | tf_op jit(solution)/shard_map/first_kernel/pallas_call | solution.py:511
  29.7 16.4 %exchange_2.1 = (f32[2,152,128]{2,1,0:T(8,128)}, f32[2,152,128]{2,1,0:T(8,128)}, f32[12,4,32,128]{3,2,1,0:T(8,128)}) custom-call(f32[4,152,128]{2,1,0:T(8,128)} %get-tuple-element.24.refs_0_, f32[4,32,128]{2,1,0:T(8,128)} %get-tuple-element.25.refs_1_), custom_call_target="tpu_custom_call" | custom-call | tf_op jit(solution)/shard_map/exchange_2/pallas_call | solution.py:490
  46.1 13.4 %second_kernel.1 = (f32[2,512,128]{2,1,0:T(8,128)}, f32[2,296,128]{2,1,0:T(8,128)}) custom-call(f32[12,4,32,128]{3,2,1,0:T(8,128)} %get-tuple-element.28.pooled, s32[96,128]{1,0:T(8,128)} %bitcast.7, s32[2,26]{1,0:T(2,128)} %links.6, f32[64,128]{1,0:T(8,128)} %bitcast.9, f32[128,3456]{1,0:T(8,128)} %weight.5, f32[1,128]{1,0:T(1,128)} %bitcast.13), custom_call_target="tpu_custom_call" | custom-call | tf_op jit(solution)/shard_map/second_kernel/pallas_call | solution.py:511
  59.4 17.8 %exchange_3.1 = (f32[2,296,128]{2,1,0:T(8,128)}, f32[2,296,128]{2,1,0:T(8,128)}) custom-call(f32[2,296,128]{2,1,0:T(8,128)} %get-tuple-element.31.refs_0_), custom_call_target="tpu_custom_call" | custom-call | tf_op jit(solution)/shard_map/exchange_3/pallas_call | solution.py:490
  77.2 10.6 %third_kernel.1.refs_0_ = f32[20,32,128]{2,1,0:T(8,128)} custom-call(f32[2,512,128]{2,1,0:T(8,128)} %get-tuple-element.30.first, f32[2,296,128]{2,1,0:T(8,128)} %get-tuple-element.32.left, f32[2,296,128]{2,1,0:T(8,128)} %get-tuple-element.33.right, s32[2,26]{1,0:T(2,128)} %links.6, s32[96,128]{1,0:T(8,128)} %bitcast.8, f32[128,3456]{1,0:T(8,128)} %weight.6, ...), custom_call_target="tpu_custom_call" | custom-call | tf_op jit(solution)/shard_map/third_kernel/pallas_call | solution.py:511
  87.7 12.9 %exchange_4.1 = (f32[4,8,32,128]{3,2,1,0:T(8,128)}, f32[4,2,32,128]{3,2,1,0:T(8,128)}, f32[4,2,32,128]{3,2,1,0:T(8,128)}) custom-call(f32[20,32,128]{2,1,0:T(8,128)} %third_kernel.1.refs_0_), custom_call_target="tpu_custom_call" | custom-call | tf_op jit(solution)/shard_map/exchange_4/pallas_call | solution.py:490
  100.6 12.1 %fourth_kernel.1 = f32[4,64,512]{2,1,0:T(8,128)} custom-call(f32[4,64,512]{2,1,0:T(8,128)} %x.7, f32[4,256,128]{2,1,0:T(8,128)} %get-tuple-element.23.hidden, f32[2,152,128]{2,1,0:T(8,128)} %get-tuple-element.26.left, f32[2,152,128]{2,1,0:T(8,128)} %get-tuple-element.27.right, f32[4,8,32,128]{3,2,1,0:T(8,128)} %get-tuple-element.34.window, ...), custom_call_target="tpu_custom_call" | custom-call | tf_op jit(solution)/shard_map/fourth_kernel/pallas_call | solution.py:511
where the time goes:
time: 113 us
  Pallas kernels  111 us (98%)
  local copies, waits for them, and re-layouts  1.25 us (1%)
    pallas_call x4, Pallas kernels, exchange(): pl.pallas_call(functools.partial(exchange_kernel, [m for _, m in halos],...  61.2 us
    pallas_call x5, Pallas kernels, local(): pl.pallas_call(kernel, out_shape=shapes, in_specs=[smem if i in scalars e...  50.3 us

commit v1 on v0

v1 whole, which is shorter than its diff:
```python
import functools

import jax
import jax.numpy as jnp
from jax import lax
from jax.experimental import pallas as pl
from jax.experimental.pallas import tpu as pltpu
from jax.sharding import PartitionSpec as P

F32 = jnp.float32
BF16 = jnp.bfloat16
MESH = pl.DeviceIdType.MESH
SIDE = 8
VOX = SIDE * SIDE * SIDE
HALO = 2
SURFACE = VOX - 6 * 6 * 6
LINE = 24
LIMIT = 62 * 1024 * 1024
CHUNKS = ((0, 96), (96, 96), (192, 104))

offsets = [(x, y, z) for x in (-1, 0, 1) for y in (-1, 0, 1) for z in (-1, 0, 1)]
columns = {o: k for k, o in enumerate(o for o in offsets if o != (0, 0, 0))}


def high_of(v):
    return v.astype(BF16).astype(F32)


def silu(v):
    return v / (1.0 + jnp.exp(-v))


def dot(a, b):
    return lax.dot_general(a, b, (((1,), (0,)), ((), ())), preferred_element_type=F32)


def first_half(v):
    return lax.broadcasted_iota(jnp.int32, v.shape, 1) < v.shape[1] // 2


def merged(a, b):
    return jnp.where(first_half(a), a, b)


def doubled(v):
    turned = pltpu.roll(v, v.shape[1] // 2, 1)
    return merged(v, turned), merged(turned, v)


def parted(v):
    high = high_of(v)
    return merged(high, v - high)


def fill(load, link, put, rims, put_rim):
    found = {o: link(o) for o in columns}

    def get(o, start, size=SIDE, stride=1):
        row, keep = found[o]
        return load(row, start, size, stride) * keep

    for px in range(SIDE + 2):
        dx = -1 if px == 0 else (1 if px == SIDE + 1 else 0)
        x = {-1: SIDE - 1, 0: px - 1, 1: 0}[dx]
        low = get((dx, -1, 0), 64 * x + 56)
        high = get((dx, 1, 0), 64 * x)
        middle = get((dx, 0, 0), 64 * x, 64) if dx else load(None, 64 * x, 64, 1)
        put(px, jnp.concatenate([low, middle, high], axis=0))
    for plane, dz in enumerate((-1, 1)):
        z = SIDE - 1 if dz < 0 else 0
        for px in range(SIDE + 2):
            dx = -1 if px == 0 else (1 if px == SIDE + 1 else 0)
            x = {-1: SIDE - 1, 0: px - 1, 1: 0}[dx]
            rims[plane, px * LINE + 8 : px * LINE + 16] = get((dx, 0, dz), 64 * x + z, SIDE, 8)
            if dx:
                for dy in (-1, 1):
                    y = SIDE - 1 if dy < 0 else 0
                    at = px * LINE + (7 if dy < 0 else 16)
                    rims[plane, at : at + 1] = get((dx, dy, dz), 64 * x + 8 * y + z, 1)
        for dy in (-1, 1):
            y = SIDE - 1 if dy < 0 else 0
            at = LINE + (7 if dy < 0 else 16)
            rims[plane, pl.ds(at, SIDE, stride=LINE)] = get((0, dy, dz), 8 * y + z, SIDE, 64)
    for j in range(3):
        for px in range(SIDE + 2):
            at = px * LINE + 7 + j
            put_rim(j, px, jnp.concatenate([rims[0, at : at + 8], rims[1, at : at + 8]], axis=0))


def stacked(even, odd, edge):
    taps = []
    for i in range(3):
        for j in range(3):
            main = odd[i : i + 8] if j == 1 else even[i : i + 8, 8 * j : 8 * j + 64]
            rim = edge[j, i : i + 8]
            taps.append(jnp.concatenate([main.reshape(VOX, 128), rim.reshape(128, 128)], axis=0))
    return jnp.concatenate(taps, axis=1)


def shifted_sum(blocks, down, up):
    before, here, after = blocks
    down[8 : VOX + 8] = before[:VOX]
    up[8 : VOX + 8] = after[:VOX]
    for x in range(SIDE):
        rim = VOX + 16 * x
        down[pl.ds(7 + 64 * x, SIDE, stride=8)] = before[rim : rim + 8]
        up[pl.ds(16 + 64 * x, SIDE, stride=8)] = after[rim + 8 : rim + 16]
    return down[7 : VOX + 7] + here[:VOX] + up[9 : VOX + 9]


def fine_matrix(weight, matrix):
    w = weight[...]
    high = high_of(w)
    both = jnp.concatenate([high, w - high], axis=0).T.astype(BF16)
    for tap in range(27):
        rows, cols = tap // 3 * 128, tap % 3 * 128
        block = both[64 * tap : 64 * tap + 64]
        matrix[rows : rows + 64, cols : cols + 128] = block
        matrix[rows + 64 : rows + 128, cols : cols + 128] = block


def coarse_matrix(weight, matrix):
    for tap in range(27):
        rows, cols = tap // 3 * 128, tap % 3 * 128
        block = weight[:, 128 * tap : 128 * tap + 128].T
        high = high_of(block)
        matrix[rows : rows + 128, cols : cols + 128] = high.astype(BF16)
        matrix[rows : rows + 128, 384 + cols : 384 + cols + 128] = (block - high).astype(BF16)


def linker(links, brick, start, own, rows):
    def link(o):
        there = links[brick, columns[o]]
        there_is = there >= 0
        row = jnp.where(there_is, jnp.clip(there - start, 0, rows - 1), own)
        return row, jnp.where(there_is, 1.0, 0.0).astype(F32)

    return link


def loader(parts, own):
    def load(row, start, size, stride):
        row = own if row is None else row
        if stride == 1:
            return parts[row, start : start + size]
        return parts[row, pl.ds(start, size, stride=stride)]

    return load


def fine_conv(parts, own, start, links, brick, scratch, matrix):
    even, odd, edge, rims, down, up = scratch

    def put(px, v):
        even[px] = v.astype(BF16)
        odd[px] = v[8:72].astype(BF16)

    def put_rim(j, px, v):
        edge[j, px] = v.astype(BF16)

    fill(loader(parts, own), linker(links, brick, start, own, parts.shape[0]), put, rims, put_rim)
    sums = dot(stacked(even, odd, edge), matrix[...])
    out = shifted_sum([sums[:, 128 * k : 128 * k + 128] for k in range(3)], down, up)
    return out + pltpu.roll(out, 64, 1)


def coarse_conv(parts, own, start, links, brick, scratch, matrix):
    even, odd, edge, rims, down, up = scratch

    def put(px, v):
        high = v.astype(BF16)
        low = (v - high.astype(F32)).astype(BF16)
        for part, value in enumerate((high, low)):
            even[part, px] = value
        middle = v[8:72]
        high = middle.astype(BF16)
        odd[0, px] = high
        odd[1, px] = (middle - high.astype(F32)).astype(BF16)

    def put_rim(j, px, v):
        high = v.astype(BF16)
        edge[0, j, px] = high
        edge[1, j, px] = (v - high.astype(F32)).astype(BF16)

    fill(loader(parts, own), linker(links, brick, start, own, parts.shape[0]), put, rims, put_rim)
    tops = dot(stacked(even.at[0], odd.at[0], edge.at[0]), matrix[...])
    rests = dot(stacked(even.at[1], odd.at[1], edge.at[1]), matrix[:, 0:384])
    cut = lambda v, at: v[:, 128 * at : 128 * at + 128]
    blocks = [cut(tops, k) + cut(tops, 3 + k) + cut(rests, k) for k in range(3)]
    return shifted_sum(blocks, down, up)


def surface_spots():
    spots = [(0, 0, 64, 1), (64, 448, 64, 1)]
    for x in range(1, 7):
        at = 128 + (x - 1) * 16
        spots += [(at, 64 * x, 8, 1), (at + 8, 64 * x + 56, 8, 1)]
    for x in range(1, 7):
        at = 224 + (x - 1) * 12
        spots += [(at, 64 * x + 8, 6, 8), (at + 6, 64 * x + 15, 6, 8)]
    return spots


def pack(get, wire):
    for at, start, size, stride in surface_spots():
        wire[at : at + size] = get(pl.ds(start, size, stride=stride) if stride > 1 else pl.ds(start, size))


def unpack(wire, brick):
    for at, start, size, stride in surface_spots():
        spot = pl.ds(start, size, stride=stride) if stride > 1 else pl.ds(start, size)
        brick[spot] = wire[at : at + size]


def unpack_pair(wire, scratch, first, second):
    a, b = doubled(wire)
    scratch[0] = parted(a)
    scratch[1] = parted(b)
    unpack(scratch.at[0], first)
    unpack(scratch.at[1], second)


def pool(v, scratch):
    lines = v.reshape(4, 2, 4, 2, SIDE, 128)
    sums = (lines[:, 0, :, 0] + lines[:, 0, :, 1]) + (lines[:, 1, :, 0] + lines[:, 1, :, 1])
    scratch[...] = sums.reshape(128, 128)
    total = scratch[pl.ds(0, 64, stride=2)] + scratch[pl.ds(1, 64, stride=2)]
    return total * 0.125


def place_piece(wire, octant, brick):
    a, b, c = octant // 4, octant // 2 % 2, octant % 2
    for half, v in enumerate(doubled(wire)):
        v = parted(v)
        for xx in range(2):
            for y in range(4):
                at = (4 * a + xx + 2 * half) * 64 + (4 * b + y) * 8 + 4 * c
                rows = xx * 16 + y * 4
                brick[at : at + 4] = v[rows : rows + 4]


def take_pieces(v, pieces):
    for a in range(2):
        for b in range(2):
            for xx in range(2):
                for y in range(4):
                    at = (4 * a + xx) * 64 + (4 * b + y) * 8
                    line = merged(v[at : at + 8], v[at + 128 : at + 136])
                    rows = xx * 16 + y * 4
                    for c in range(2):
                        pieces[4 * a + 2 * b + c, rows : rows + 4] = line[4 * c : 4 * c + 4]


def grow(piece, scratch):
    for half, v in enumerate(doubled(piece)):
        for xx in range(2):
            for y in range(2):
                rows = v[xx * 16 + y * 8 : xx * 16 + y * 8 + 8]
                at = ((2 * half + xx) * 2 + y) * 16
                scratch[pl.ds(at, 8, stride=2)] = rows
                scratch[pl.ds(at + 1, 8, stride=2)] = rows
    lines = scratch[...].reshape(4, 1, 4, 1, SIDE, 128)
    return jnp.broadcast_to(lines, (4, 2, 4, 2, SIDE, 128)).reshape(VOX, 128)


def step_kernel(
    x_any, fine_links, own_codes, coarse_links, in_any, in_bias, down_weight, one_any, one_bias, two_any, two_bias,
    up_weight, out_any, out_bias,
    out,
    x, in_weight, one_weight, two_weight, out_weight, loads,
    matrix, last_matrix, one_matrix, two_matrix,
    even, odd, edge, wide_even, wide_odd, wide_edge, rims, shift_down, shift_up,
    parts, turned, hidden, halves, small, grown,
    x_send, x_halo, hidden_send, hidden_halo,
    code_block, codes, code_table, table, code_scalars, table_scalars,
    pooled, placed, base, first,
    first_send, first_halo, lifted, wanted, window, low_window, high_window,
    local_sems, send_x, recv_x, send_hidden, recv_hidden, send_codes, recv_codes, send_pooled, recv_pooled,
    send_first, recv_first, send_relay, recv_relay, send_wanted, recv_wanted,
):
    group, member = lax.axis_index("grp"), lax.axis_index("dev")
    groups, members = lax.axis_size("grp"), lax.axis_size("dev")
    position = group * members + member
    whole = groups * members
    count, slots = fine_links.shape[0], coarse_links.shape[0]
    pairs = count // 2
    relayed = members == 4
    has_left, has_right = position > 0, position < whole - 1
    has_low, has_high = group > 0, group < groups - 1
    is_first, is_last = member == 0, member == members - 1
    left_at = (jnp.maximum(position - 1, 0) // members, (position + members - 1) % members)
    right_at = (jnp.minimum(position + 1, whole - 1) // members, (position + 1) % members)
    low_at = (jnp.maximum(group - 1, 0), members - 1)
    high_at = (jnp.minimum(group + 1, groups - 1), 0)
    always = position >= 0

    def fetch(k, source, target):
        return pltpu.make_async_copy(source, target, loads.at[k])

    fetches = [
        fetch(0, x_any, x), fetch(1, in_any, in_weight), fetch(2, one_any, one_weight),
        fetch(3, two_any, two_weight), fetch(4, out_any, out_weight),
    ]
    for copy in fetches:
        copy.start()

    barrier = pltpu.get_barrier_semaphore()

    def greet(where):
        pl.semaphore_signal(barrier, inc=1, device_id=where, device_id_type=MESH)

    pl.when(has_left)(lambda: greet(left_at))
    pl.when(has_right)(lambda: greet(right_at))
    for k in range(1, members):
        greet((group, (member + k) % members))
    for k in range(members):
        pl.when(is_first & has_low)(lambda k=k: greet((low_at[0], k)))
        pl.when(is_last & has_high)(lambda k=k: greet((high_at[0], k)))

    def remote(src, dst, send, recv, where):
        return pltpu.make_async_remote_copy(
            src_ref=src, dst_ref=dst, send_sem=send, recv_sem=recv, device_id=where, device_id_type=MESH
        )

    row = lax.broadcasted_iota(jnp.int32, (SIDE, 128), 0)
    block = jnp.full((SIDE, 128), -1, jnp.int32)
    for i in range(count):
        block = jnp.where(row == i, own_codes[i], block)
    code_block[...] = block
    codes[members + member] = block
    fetches[0].wait()
    for pair in range(pairs):
        turned[pair] = x[2 * pair : 2 * pair + 2].reshape(128, VOX).T
    pack(lambda spot: turned[0, spot], x_send.at[0])
    pack(lambda spot: turned[pairs - 1, spot], x_send.at[1])
    pl.semaphore_wait(
        barrier,
        jnp.where(has_left, 1, 0) + jnp.where(has_right, 1, 0) + (members - 1)
        + jnp.where(has_low, 1, 0) + jnp.where(has_high, 1, 0),
    )

    def halo_copies(source, halo, send, recv):
        to_left = remote(source.at[0], halo.at[1], send.at[0], recv.at[1], left_at)
        to_right = remote(source.at[1], halo.at[0], send.at[1], recv.at[0], right_at)
        return to_left, to_right

    def start_halo(copies):
        pl.when(has_left)(copies[0].start)
        pl.when(has_right)(copies[1].start)

    def end_halo(copies):
        pl.when(has_left)(copies[1].wait_recv)
        pl.when(has_right)(copies[0].wait_recv)

    def end_halo_sends(copies):
        pl.when(has_left)(copies[0].wait_send)
        pl.when(has_right)(copies[1].wait_send)

    def shared_copies(source, at, send, recv):
        near = [
            remote(source, at(members + member), send.at[k], recv.at[members + member], (group, (member + k) % members))
            for k in range(1, members)
        ]
        to_high = remote(source, at(member), send.at[0], recv.at[member], high_at)
        to_low = remote(source, at(2 * members + member), send.at[members], recv.at[2 * members + member], low_at)
        return near, to_high, to_low

    def start_shared(copies):
        near, to_high, to_low = copies
        for copy in near:
            copy.start()
        pl.when(has_high)(to_high.start)
        pl.when(has_low)(to_low.start)

    def end_shared(source, at, send, recv):
        for k in range(1, members):
            other = (member + k) % members
            remote(source, at(members + other), send.at[k], recv.at[members + other], (group, other)).wait_recv()
        for k in range(members):
            from_low = remote(source, at(k), send.at[0], recv.at[k], low_at)
            from_high = remote(source, at(2 * members + k), send.at[0], recv.at[2 * members + k], high_at)
            pl.when(is_first & has_low)(from_low.wait_recv)
            pl.when(is_last & has_high)(from_high.wait_recv)

    def end_shared_sends(copies):
        near, to_high, to_low = copies
        for copy in near:
            copy.wait_send()
        pl.when(has_high)(to_high.wait_send)
        pl.when(has_low)(to_low.wait_send)

    x_copies = halo_copies(x_send, x_halo, send_x, recv_x)
    start_halo(x_copies)
    code_at = lambda k: codes.at[k]
    code_copies = shared_copies(code_block, code_at, send_codes, recv_codes)
    start_shared(code_copies)

    fetches[1].wait()
    fine_matrix(in_weight, matrix)
    for pair in range(pairs):
        for one, v in enumerate(doubled(turned[pair])):
            parts[HALO + 2 * pair + one] = parted(v)
    end_shared(code_block, code_at, send_codes, recv_codes)
    lane = lax.broadcasted_iota(jnp.int32, (SIDE, 128), 1)
    table_rows = jnp.full((SIDE, 128), -1, jnp.int32)
    for near in range(3):
        there = position + near - 1
        valid = (there >= 0) & (there < whole)
        there = jnp.where(valid, there, position)
        there_group = there // members
        there_member = there - there_group * members
        band = there_group - group + 1
        spot = jnp.where(valid, lane, -1000) + there_member * slots * 8
        best = jnp.full((SIDE, 128), -1, jnp.int32)
        for k in range(members):
            match = (codes[band * members + k] == spot) & (row < count) & (lane < slots * 8)
            best = jnp.maximum(best, jnp.where(match, (band * members + k) * count + row, -1))
        top = jnp.max(best, axis=0, keepdims=True)
        table_rows = jnp.where(row == near, top, table_rows)
    code_table[...] = codes[pl.ds(members, members)]
    table[...] = table_rows
    to_table = pltpu.make_async_copy(table, table_scalars, local_sems.at[0])
    to_codes = pltpu.make_async_copy(code_table, code_scalars, local_sems.at[1])
    to_table.start()
    to_codes.start()
    fetches[2].wait()
    coarse_matrix(one_weight, one_matrix)
    fetches[3].wait()
    coarse_matrix(two_weight, two_matrix)
    fetches[4].wait()
    fine_matrix(out_weight, last_matrix)
    to_table.wait()
    to_codes.wait()

    fine_start = position * count - HALO
    end_halo(x_copies)
    for side, at in ((0, 0), (1, HALO + count)):
        unpack_pair(x_halo[side], halves, parts.at[at], parts.at[at + 1])
    fine_scratch = (even, odd, edge, rims, shift_down, shift_up)
    two = lambda bias: jnp.concatenate([bias[...], bias[...]], axis=1)
    in_both = two(in_bias)

    def pooled_at(i):
        return lambda k: pooled.at[k, i]

    def pooled_copies(i):
        return shared_copies(pooled.at[members + member, i], pooled_at(i), send_pooled.at[i], recv_pooled.at[i])

    def first_step(i, carry):
        v = silu(fine_conv(parts, HALO + i, fine_start, fine_links, i, fine_scratch, matrix) + in_both)
        means = pool(v, small)
        pooled[members + member, i] = merged(means[0:32], means[32:64])
        hidden[i] = v
        start_shared(pooled_copies(i))
        return carry

    lax.fori_loop(0, count, first_step, 0)
    pack(lambda spot: merged(hidden[0, spot], hidden[1, spot]), hidden_send.at[0])
    pack(lambda spot: merged(hidden[count - 2, spot], hidden[count - 1, spot]), hidden_send.at[1])
    hidden_copies = halo_copies(hidden_send, hidden_halo, send_hidden, recv_hidden)
    start_halo(hidden_copies)

    turned_down = down_weight[...].T
    down_high = high_of(turned_down)
    down_both = jnp.concatenate([down_high, turned_down - down_high], axis=1)
    down_matrix = jnp.concatenate([down_both, down_both], axis=0).astype(BF16)
    for i in range(count):
        end_shared(pooled.at[members + member, i], pooled_at(i), send_pooled.at[i], recv_pooled.at[i])

    def base_step(slot, carry):
        for octant in range(8):
            which = table_scalars[slot // slots, slot % slots * 8 + octant]
            there_is = which >= 0
            which = jnp.where(there_is, jnp.minimum(which, 3 * members * count - 1), (members + member) * count)
            keep = jnp.where(there_is, 1.0, 0.0).astype(F32)
            place_piece(pooled[which // count, which % count] * keep, octant, placed)
        sums = dot(placed[...].astype(BF16), down_matrix)
        base[slot] = sums[:, 0:128] + sums[:, 128:256]
        return carry

    lax.fori_loop(0, 3 * slots, base_step, 0)
    coarse_start = (position - 1) * slots
    wide_scratch = (wide_even, wide_odd, wide_edge, rims, shift_down, shift_up)

    if relayed:
        parity = member % 2
        x_at = (group, member + 1 - 2 * parity)
        relay_group = group + jnp.where(member == 1, -1, 0) + jnp.where(member == 2, 1, 0)
        relays_out = (relay_group >= 0) & (relay_group < groups)
        relays_in = jnp.where(is_first, has_low, True) & jnp.where(is_last, has_high, True)
        relay_at = (jnp.clip(relay_group, 0, groups - 1), (member + 2) % members)

        def direct(i, c):
            at, rows = CHUNKS[c]
            return remote(
                first_send.at[i, pl.ds(at, rows)], first_halo.at[parity, i, pl.ds(at, rows)],
                send_first.at[i, c], recv_first.at[i, c], x_at,
            )

        def came(i, c):
            at, rows = CHUNKS[c]
            return remote(
                first_send.at[i, pl.ds(at, rows)], first_halo.at[1 - parity, i, pl.ds(at, rows)],
                send_first.at[i, c], recv_first.at[i, c], x_at,
            )

        def relay(i, c):
            at, rows = CHUNKS[c]
            return remote(
                first_halo.at[1 - parity, i, pl.ds(at, rows)], first_halo.at[parity, i, pl.ds(at, rows)],
                send_relay.at[i, c], recv_relay.at[i, c], relay_at,
            )

        def start_first(i):
            for c in range(len(CHUNKS)):
                direct(i, c).start()

        def end_first():
            for i in range(slots):
                for c in range(len(CHUNKS)):
                    came(i, c).wait_recv()
                    pl.when(relays_out)(relay(i, c).start)
            for i in range(slots):
                for c in range(len(CHUNKS)):
                    pl.when(relays_in)(relay(i, c).wait_recv)

        def end_first_sends():
            for i in range(slots):
                for c in range(len(CHUNKS)):
                    direct(i, c).wait_send()
                    pl.when(relays_out)(relay(i, c).wait_send)
    else:

        def sides(i):
            to_left = remote(first_send.at[i], first_halo.at[1, i], send_first.at[i, 0], recv_first.at[i, 1], left_at)
            to_right = remote(first_send.at[i], first_halo.at[0, i], send_first.at[i, 1], recv_first.at[i, 0], right_at)
            return to_left, to_right

        def start_first(i):
            start_halo(sides(i))

        def end_first():
            for i in range(slots):
                end_halo(sides(i))

        def end_first_sends():
            for i in range(slots):
                end_halo_sends(sides(i))

    def second_step(i, carry):
        v = silu(coarse_conv(base, slots + i, coarse_start, coarse_links, i, wide_scratch, one_matrix) + one_bias[...])
        first[slots + i] = v
        pack(lambda spot: first[slots + i, spot], first_send.at[i])
        start_first(i)
        return carry

    lax.fori_loop(0, slots, second_step, 0)
    turned_up = up_weight[...].T
    up_high = high_of(turned_up)
    up_both = jnp.concatenate([up_high, turned_up - up_high], axis=1)
    up_matrix = jnp.concatenate([up_both, up_both], axis=0).astype(BF16)
    end_first()
    for side, at in ((0, 0), (1, 2 * slots)):
        for i in range(slots):
            unpack(first_halo.at[side, i], first.at[at + i])

    def third_step(i, carry):
        v = silu(coarse_conv(first, slots + i, coarse_start, coarse_links, i, wide_scratch, two_matrix) + two_bias[...])
        high = v.astype(BF16)
        low = (v - high.astype(F32)).astype(BF16)
        sums = dot(jnp.concatenate([high, low], axis=1), up_matrix)
        take_pieces(sums + pltpu.roll(sums, 64, 1), lifted.at[pl.ds(i * 8, 8)])
        return carry

    lax.fori_loop(0, slots, third_step, 0)
    bricks = members * count
    zeros = jnp.zeros((HALO,) + wanted.shape[1:], F32)
    wanted[0:HALO] = zeros
    wanted[HALO + bricks :] = zeros

    def choose(j, carry):
        code = code_scalars[j // count, j % count, 0] - member * slots * 8
        mine = (code >= 0) & (code < slots * 8)
        keep = jnp.where(mine, 1.0, 0.0).astype(F32)
        wanted[HALO + j] = lifted[jnp.where(mine, code, 0)] * keep
        return carry

    lax.fori_loop(0, bricks, choose, 0)
    span = count + 2 * HALO

    def to_member(k):
        other = (member + k) % members
        return remote(
            wanted.at[pl.ds(other * count, span)], window.at[member], send_wanted.at[k],
            recv_wanted.at[members + member], (group, other),
        )

    to_high = remote(
        wanted.at[pl.ds(bricks, HALO)], low_window.at[member], send_wanted.at[0], recv_wanted.at[member], high_at
    )
    to_low = remote(
        wanted.at[pl.ds(HALO, HALO)], high_window.at[member], send_wanted.at[members],
        recv_wanted.at[2 * members + member], low_at,
    )
    for k in range(1, members):
        to_member(k).start()
    pl.when(has_high)(to_high.start)
    pl.when(has_low)(to_low.start)
    window[member] = wanted[pl.ds(member * count, span)]
    end_halo(hidden_copies)
    for k in range(1, members):
        other = (member + k) % members
        remote(
            wanted.at[pl.ds(0, span)], window.at[other], send_wanted.at[k], recv_wanted.at[members + other],
            (group, other),
        ).wait_recv()
    for k in range(members):
        from_low = remote(wanted.at[pl.ds(0, HALO)], low_window.at[k], send_wanted.at[0], recv_wanted.at[k], low_at)
        from_high = remote(
            wanted.at[pl.ds(0, HALO)], high_window.at[k], send_wanted.at[0], recv_wanted.at[2 * members + k], high_at
        )
        pl.when(is_first & has_low)(from_low.wait_recv)
        pl.when(is_last & has_high)(from_high.wait_recv)

    def total(source, i):
        piece = source[0, i]
        for owner in range(1, members):
            piece = piece + source[owner, i]
        return piece

    def own_blend(i, carry):
        rising = grow(total(window, HALO + i), small)
        parts[HALO + i] = parted(silu(hidden[i] + rising))
        return carry

    lax.fori_loop(0, count, own_blend, 0)
    for side, at, edge_window, beyond in (
        (0, 0, low_window, is_first), (1, HALO + count, high_window, is_last),
    ):
        for one in range(HALO):
            piece = jnp.where(beyond, total(edge_window, one), total(window, at + one))
            grown[one] = grow(piece, small)
        pack(lambda spot: merged(grown[0, spot], grown[1, spot]), halves.at[0])
        wire = silu(hidden_halo[side] + halves[0])
        unpack_pair(wire, halves, parts.at[at], parts.at[at + 1])
    out_both = two(out_bias)

    def last_step(i, carry):
        hidden[i] = fine_conv(parts, HALO + i, fine_start, fine_links, i, fine_scratch, last_matrix) + out_both
        return carry

    lax.fori_loop(0, count, last_step, 0)
    for pair in range(pairs):
        flat = merged(hidden[2 * pair], hidden[2 * pair + 1]).T
        out[2 * pair : 2 * pair + 2] = x[2 * pair : 2 * pair + 2] + flat.reshape(2, 64, VOX)

    end_halo_sends(x_copies)
    end_shared_sends(code_copies)
    for i in range(count):
        end_shared_sends(pooled_copies(i))
    end_halo_sends(hidden_copies)
    end_first_sends()
    for k in range(1, members):
        to_member(k).wait_send()
    pl.when(has_high)(to_high.wait_send)
    pl.when(has_low)(to_low.wait_send)


def per_device(
    x, fine_links, parent_codes, coarse_links,
    in_weight, in_bias, down, one_weight, one_bias, two_weight, two_bias, up, out_weight, out_bias,
):
    count, channels = x.shape[0], x.shape[1]
    slots, wide = coarse_links.shape[0], one_bias.shape[0]
    members = lax.axis_size("dev")
    row = lambda bias: bias.reshape(1, -1)
    vmem = pl.BlockSpec(memory_space=pltpu.VMEM)
    smem = pl.BlockSpec(memory_space=pltpu.SMEM)
    anywhere = pl.BlockSpec(memory_space=pl.ANY)
    floats = lambda *shape: pltpu.VMEM(shape, F32)
    halfs = lambda *shape: pltpu.VMEM(shape, BF16)
    ints = lambda *shape: pltpu.VMEM(shape, jnp.int32)
    sems = lambda *shape: pltpu.SemaphoreType.DMA(shape)
    span = count + 2 * HALO
    wire = (32, 128)
    scratch = [
        floats(*x.shape), floats(*in_weight.shape), floats(*one_weight.shape), floats(*two_weight.shape),
        floats(*out_weight.shape), sems(5),
        halfs(1152, 384), halfs(1152, 384), halfs(1152, 768), halfs(1152, 768),
        halfs(10, 80, 128), halfs(10, 64, 128), halfs(3, 10, 16, 128),
        halfs(2, 10, 80, 128), halfs(2, 10, 64, 128), halfs(2, 3, 10, 16, 128),
        floats(2, 10 * LINE, 128), floats(VOX + 16, 128), floats(VOX + 16, 128),
        floats(span, VOX, 128), floats(count // 2, VOX, 128), floats(count, VOX, 128),
        floats(2, SURFACE, 128), floats(128, 128), floats(HALO, VOX, 128),
        floats(2, SURFACE, 128), floats(2, SURFACE, 128), floats(2, SURFACE, 128), floats(2, SURFACE, 128),
        ints(8, 128), ints(3 * members, 8, 128), ints(members, 8, 128), ints(8, 128),
        pltpu.SMEM((members, 8, 128), jnp.int32), pltpu.SMEM((8, 128), jnp.int32),
        floats(3 * members, count, *wire), floats(VOX, 128), floats(3 * slots, VOX, 128), floats(3 * slots, VOX, 128),
        floats(slots, SURFACE, 128), floats(2, slots, SURFACE, 128), floats(slots * 8, *wire),
        floats(members * count + 2 * HALO, *wire), floats(members, span, *wire), floats(members, HALO, *wire),
        floats(members, HALO, *wire),
        sems(2), sems(2), sems(2), sems(2), sems(2), sems(members + 1), sems(3 * members),
        sems(count, members + 1), sems(count, 3 * members),
        sems(slots, 3), sems(slots, 3), sems(slots, 3), sems(slots, 3), sems(members + 1), sems(3 * members),
    ]
    return pl.pallas_call(
        step_kernel,
        out_shape=jax.ShapeDtypeStruct(x.shape, F32),
        in_specs=[anywhere, smem, smem, smem, anywhere, vmem, vmem, anywhere, vmem, anywhere, vmem, vmem, anywhere, vmem],
        out_specs=vmem,
        scratch_shapes=scratch,
        name="step",
        compiler_params=pltpu.CompilerParams(collective_id=1, has_side_effects=True, vmem_limit_bytes=LIMIT),
    )(
        x, fine_links, parent_codes, coarse_links, in_weight, row(in_bias), down, one_weight, row(one_bias),
        two_weight, row(two_bias), up, out_weight, row(out_bias),
    )


def solution(mesh):
    bricks = P(("grp", "dev"), None, None)
    rows = P(("grp", "dev"), None)
    placed = (bricks, rows, P(("grp", "dev")), rows) + (P(),) * 10
    return jax.shard_map(per_device, mesh=mesh, in_specs=placed, out_specs=bricks, check_vma=False)
```

time: 113 us -> 66.3 us (0.59)
  Pallas kernels: 111 us -> 62.2 us
  local copies, waits for them, and re-layouts: 1.25 us -> 3.35 us
    pallas_call x9 -> x1, Pallas kernels: 111 us -> 62.2 us  [per_device(): pl.pallas_call(step_kernel, out_shape=jax.ShapeDtypeStruct(x.shape, F32),...]
    unnamed x0 -> x2, local copies, waits for them, and re-layouts: none -> 3.35 us
    pad x1 -> x0, local copies, waits for them, and re-layouts: 1.25 us -> none  [per_device(): jnp.pad(parent_codes.reshape(1, -1), ((0, 7), (0, 128 - count)))]
where the time goes in v1:
time: 66.3 us; the launch traced here: 65.5 us
  Pallas kernels  62.2 us (94%)
  local copies, waits for them, and re-layouts  3.35 us (5%)
    pallas_call x1, Pallas kernels, per_device(): pl.pallas_call(step_kernel, out_shape=jax.ShapeDtypeStruct(x.shape, F32),...  62.2 us
    unnamed x2, local copies, waits for them, and re-layouts  3.35 us

profile of v1, /device:TPU:0, one launch (start us, length us, event | category | flops | bytes accessed | tf_op | source)
XLA Modules:
  0.0 65.5 jit_solution(5710502848295901401)
XLA Ops:
  0.0 1.5 %copy.15.down_weight = f32[128,64]{1,0:T(8,128)} copy(f32[128,64]{0,1:T(8,128)} %param.20) | data formatting | bytes 65536 | tf_op args[6]
  1.5 62.2 %step.1 = f32[4,64,512]{2,1,0:T(8,128)} custom-call(f32[4,64,512]{2,1,0:T(8,128)} %x_any.1, s32[4,26]{1,0:T(4,128)} %fine_links.1, s32[4]{0:T(128)} %own_codes.1, s32[2,26]{1,0:T(2,128)} %coarse_links.1, f32[64,1728]{1,0:T(8,128)} %in_any.1, f32[1,64]{1,0:T(1,128)} %bitcast.4, f32[128,64]{1,0:T(8,128)} %copy.15.down_weight, f32[128,3456]{1,0:T(8,128)} %one_any.1, ...), custom_call_target="tpu_custom_call" | custom-call | tf_op jit(solution)/shard_map/step/pallas_call | solution.py:706
  63.7 1.9 %copy.17 = f32[4,64,512]{2,1,0:T(8,128)} copy(f32[4,64,512]{2,1,0:T(8,128)} %step.1) | data formatting | bytes 1048576

commit v2 on v1

--- a/solution.py
+++ b/solution.py
@@ -220,45 +220,48 @@
     unpack(scratch.at[1], second)
 
 
-def pool(v, scratch):
+def pool(v, scratch, wire):
     lines = v.reshape(4, 2, 4, 2, SIDE, 128)
     sums = (lines[:, 0, :, 0] + lines[:, 0, :, 1]) + (lines[:, 1, :, 0] + lines[:, 1, :, 1])
     scratch[...] = sums.reshape(128, 128)
-    total = scratch[pl.ds(0, 64, stride=2)] + scratch[pl.ds(1, 64, stride=2)]
-    return total * 0.125
+    for z in range(4):
+        halves = [
+            scratch[pl.ds(64 * half + 2 * z, 8, stride=8)] + scratch[pl.ds(64 * half + 2 * z + 1, 8, stride=8)]
+            for half in range(2)
+        ]
+        wire[8 * z : 8 * z + 8] = merged(*halves) * 0.125
+
+
+def split_spot(octant, half, z):
+    a, b, c = octant // 4, octant // 2 % 2, octant % 2
+    return pl.ds(256 * b + 32 * (4 * a + 2 * half) + 4 * c + z, 8, stride=8)
 
 
 def place_piece(wire, octant, brick):
-    a, b, c = octant // 4, octant // 2 % 2, octant % 2
     for half, v in enumerate(doubled(wire)):
         v = parted(v)
-        for xx in range(2):
-            for y in range(4):
-                at = (4 * a + xx + 2 * half) * 64 + (4 * b + y) * 8 + 4 * c
-                rows = xx * 16 + y * 4
-                brick[at : at + 4] = v[rows : rows + 4]
-
-
-def take_pieces(v, pieces):
-    for a in range(2):
-        for b in range(2):
-            for xx in range(2):
-                for y in range(4):
-                    at = (4 * a + xx) * 64 + (4 * b + y) * 8
-                    line = merged(v[at : at + 8], v[at + 128 : at + 136])
-                    rows = xx * 16 + y * 4
-                    for c in range(2):
-                        pieces[4 * a + 2 * b + c, rows : rows + 4] = line[4 * c : 4 * c + 4]
+        for z in range(4):
+            brick[split_spot(octant, half, z)] = v[8 * z : 8 * z + 8]
+
+
+def take_pieces(brick, pieces):
+    for octant in range(8):
+        for z in range(4):
+            halves = [brick[split_spot(octant, half, z)] for half in range(2)]
+            pieces[octant, 8 * z : 8 * z + 8] = merged(*halves)
+
+
+def swap_halves(v, split):
+    first, second = (2, SIDE) if split else (SIDE, 2)
+    return v.reshape(first, second, 32, 128).swapaxes(0, 1).reshape(VOX, 128)
 
 
 def grow(piece, scratch):
     for half, v in enumerate(doubled(piece)):
-        for xx in range(2):
-            for y in range(2):
-                rows = v[xx * 16 + y * 8 : xx * 16 + y * 8 + 8]
-                at = ((2 * half + xx) * 2 + y) * 16
-                scratch[pl.ds(at, 8, stride=2)] = rows
-                scratch[pl.ds(at + 1, 8, stride=2)] = rows
+        for z in range(4):
+            rows = v[8 * z : 8 * z + 8]
+            scratch[pl.ds(64 * half + 2 * z, 8, stride=8)] = rows
+            scratch[pl.ds(64 * half + 2 * z + 1, 8, stride=8)] = rows
     lines = scratch[...].reshape(4, 1, 4, 1, SIDE, 128)
     return jnp.broadcast_to(lines, (4, 2, 4, 2, SIDE, 128)).reshape(VOX, 128)
 
@@ -448,8 +451,7 @@
 
     def first_step(i, carry):
         v = silu(fine_conv(parts, HALO + i, fine_start, fine_links, i, fine_scratch, matrix) + in_both)
-        means = pool(v, small)
-        pooled[members + member, i] = merged(means[0:32], means[32:64])
+        pool(v, small, pooled.at[members + member, i])
         hidden[i] = v
         start_shared(pooled_copies(i))
         return carry
@@ -460,7 +462,7 @@
     hidden_copies = halo_copies(hidden_send, hidden_halo, send_hidden, recv_hidden)
     start_halo(hidden_copies)
 
-    turned_down = down_weight[...].T
+    turned_down = down_weight[...]
     down_high = high_of(turned_down)
     down_both = jnp.concatenate([down_high, turned_down - down_high], axis=1)
     down_matrix = jnp.concatenate([down_both, down_both], axis=0).astype(BF16)
@@ -475,7 +477,7 @@
             keep = jnp.where(there_is, 1.0, 0.0).astype(F32)
             place_piece(pooled[which // count, which % count] * keep, octant, placed)
         sums = dot(placed[...].astype(BF16), down_matrix)
-        base[slot] = sums[:, 0:128] + sums[:, 128:256]
+        base[slot] = swap_halves(sums[:, 0:128] + sums[:, 128:256], True)
         return carry
 
     lax.fori_loop(0, 3 * slots, base_step, 0)
@@ -569,7 +571,8 @@
         high = v.astype(BF16)
         low = (v - high.astype(F32)).astype(BF16)
         sums = dot(jnp.concatenate([high, low], axis=1), up_matrix)
-        take_pieces(sums + pltpu.roll(sums, 64, 1), lifted.at[pl.ds(i * 8, 8)])
+        placed[...] = swap_halves(sums + pltpu.roll(sums, 64, 1), False)
+        take_pieces(placed, lifted.at[pl.ds(i * 8, 8)])
         return carry
 
     lax.fori_loop(0, slots, third_step, 0)
@@ -586,41 +589,49 @@
         return carry
 
     lax.fori_loop(0, bricks, choose, 0)
-    span = count + 2 * HALO
-
-    def to_member(k):
+    parts_of = ((HALO, count, None), (0, HALO, 0), (HALO + count, HALO, members - 1))
+
+    def to_member(k, part):
         other = (member + k) % members
+        at, rows, _ = parts_of[part]
         return remote(
-            wanted.at[pl.ds(other * count, span)], window.at[member], send_wanted.at[k],
-            recv_wanted.at[members + member], (group, other),
+            wanted.at[pl.ds(other * count + at, rows)], window.at[member, pl.ds(at, rows)], send_wanted.at[k, part],
+            recv_wanted.at[members + member, part], (group, other),
         )
 
+    def from_member(k, part):
+        other = (member + k) % members
+        at, rows, _ = parts_of[part]
+        return remote(
+            wanted.at[pl.ds(at, rows)], window.at[other, pl.ds(at, rows)], send_wanted.at[k, part],
+            recv_wanted.at[members + other, part], (group, other),
+        )
+
+    def when_read(who, part, action):
+        none_at = parts_of[part][2]
+        if none_at is None:
+            action()
+        else:
+            pl.when(who != none_at)(action)
+
     to_high = remote(
-        wanted.at[pl.ds(bricks, HALO)], low_window.at[member], send_wanted.at[0], recv_wanted.at[member], high_at
+        wanted.at[pl.ds(bricks, HALO)], low_window.at[member], send_wanted.at[0, 0], recv_wanted.at[member, 0], high_at
     )
     to_low = remote(
-        wanted.at[pl.ds(HALO, HALO)], high_window.at[member], send_wanted.at[members],
-        recv_wanted.at[2 * members + member], low_at,
+        wanted.at[pl.ds(HALO, HALO)], high_window.at[member], send_wanted.at[members, 0],
+        recv_wanted.at[2 * members + member, 0], low_at,
     )
     for k in range(1, members):
-        to_member(k).start()
+        to_member(k, 0).start()
+    for k in range(1, members):
+        for part in (1, 2):
+            when_read((member + k) % members, part, to_member(k, part).start)
     pl.when(has_high)(to_high.start)
     pl.when(has_low)(to_low.start)
-    window[member] = wanted[pl.ds(member * count, span)]
+    window[member] = wanted[pl.ds(member * count, count + 2 * HALO)]
     end_halo(hidden_copies)
     for k in range(1, members):
-        other = (member + k) % members
-        remote(
-            wanted.at[pl.ds(0, span)], window.at[other], send_wanted.at[k], recv_wanted.at[members + other],
-            (group, other),
-        ).wait_recv()
-    for k in range(members):
-        from_low = remote(wanted.at[pl.ds(0, HALO)], low_window.at[k], send_wanted.at[0], recv_wanted.at[k], low_at)
-        from_high = remote(
-            wanted.at[pl.ds(0, HALO)], high_window.at[k], send_wanted.at[0], recv_wanted.at[2 * members + k], high_at
-        )
-        pl.when(is_first & has_low)(from_low.wait_recv)
-        pl.when(is_last & has_high)(from_high.wait_recv)
+        from_member(k, 0).wait_recv()
 
     def total(source, i):
         piece = source[0, i]
@@ -634,6 +645,17 @@
         return carry
 
     lax.fori_loop(0, count, own_blend, 0)
+    for k in range(1, members):
+        for part in (1, 2):
+            when_read(member, part, from_member(k, part).wait_recv)
+    for k in range(members):
+        spot = wanted.at[pl.ds(0, HALO)]
+        from_low = remote(spot, low_window.at[k], send_wanted.at[0, 0], recv_wanted.at[k, 0], low_at)
+        from_high = remote(
+            spot, high_window.at[k], send_wanted.at[0, 0], recv_wanted.at[2 * members + k, 0], high_at
+        )
+        pl.when(is_first & has_low)(from_low.wait_recv)
+        pl.when(is_last & has_high)(from_high.wait_recv)
     for side, at, edge_window, beyond in (
         (0, 0, low_window, is_first), (1, HALO + count, high_window, is_last),
     ):
@@ -661,7 +683,9 @@
     end_halo_sends(hidden_copies)
     end_first_sends()
     for k in range(1, members):
-        to_member(k).wait_send()
+        to_member(k, 0).wait_send()
+        for part in (1, 2):
+            when_read((member + k) % members, part, to_member(k, part).wait_send)
     pl.when(has_high)(to_high.wait_send)
     pl.when(has_low)(to_low.wait_send)
 
@@ -701,7 +725,7 @@
         floats(members, HALO, *wire),
         sems(2), sems(2), sems(2), sems(2), sems(2), sems(members + 1), sems(3 * members),
         sems(count, members + 1), sems(count, 3 * members),
-        sems(slots, 3), sems(slots, 3), sems(slots, 3), sems(slots, 3), sems(members + 1), sems(3 * members),
+        sems(slots, 3), sems(slots, 3), sems(slots, 3), sems(slots, 3), sems(members + 1, 3), sems(3 * members, 3),
     ]
     return pl.pallas_call(
         step_kernel,
@@ -712,7 +736,7 @@
         name="step",
         compiler_params=pltpu.CompilerParams(collective_id=1, has_side_effects=True, vmem_limit_bytes=LIMIT),
     )(
-        x, fine_links, parent_codes, coarse_links, in_weight, row(in_bias), down, one_weight, row(one_bias),
+        x, fine_links, parent_codes, coarse_links, in_weight, row(in_bias), down.T, one_weight, row(one_bias),
         two_weight, row(two_bias), up, out_weight, row(out_bias),
     )
 

time: 66.3 us -> 63.5 us (0.958)
  local copies, waits for them, and re-layouts: 3.35 us -> 1.87 us
  Pallas kernels: 62.2 us -> 61 us
    unnamed x2 -> x1, local copies, waits for them, and re-layouts: 3.35 us -> 1.87 us
    pallas_call x1, Pallas kernels: 62.2 us -> 61 us  [per_device(): pl.pallas_call(step_kernel, out_shape=jax.ShapeDtypeStruct(x.shape, F32),...]
where the time goes in v2:
time: 63.5 us; the launch traced here: 62.8 us
  Pallas kernels  61 us (96%)
  local copies, waits for them, and re-layouts  1.87 us (3%)
    pallas_call x1, Pallas kernels, per_device(): pl.pallas_call(step_kernel, out_shape=jax.ShapeDtypeStruct(x.shape, F32),...  61 us
    unnamed x1, local copies, waits for them, and re-layouts  1.87 us

profile of v2, /device:TPU:0, one launch (start us, length us, event | category | flops | bytes accessed | tf_op | source)
XLA Modules:
  0.0 62.8 jit_solution(16763220040171990110)
XLA Ops:
  0.0 61.0 %step.1 = f32[4,64,512]{2,1,0:T(8,128)} custom-call(f32[4,64,512]{2,1,0:T(8,128)} %x_any.1, s32[4,26]{1,0:T(4,128)} %fine_links.1, s32[4]{0:T(128)} %own_codes.1, s32[2,26]{1,0:T(2,128)} %coarse_links.1, f32[64,1728]{1,0:T(8,128)} %in_any.1, f32[1,64]{1,0:T(1,128)} %bitcast.6, f32[64,128]{1,0:T(8,128)} %bitcast.5, f32[128,3456]{1,0:T(8,128)} %one_any.1, ...), custom_call_target="tpu_custom_call" | custom-call | tf_op jit(solution)/shard_map/step/pallas_call | solution.py:730
  61.0 1.9 %copy.16 = f32[4,64,512]{2,1,0:T(8,128)} copy(f32[4,64,512]{2,1,0:T(8,128)} %step.1) | data formatting | bytes 1048576

commit v3 on v2

--- a/solution.py
+++ b/solution.py
@@ -66,6 +66,10 @@
         high = get((dx, 1, 0), 64 * x)
         middle = get((dx, 0, 0), 64 * x, 64) if dx else load(None, 64 * x, 64, 1)
         put(px, jnp.concatenate([low, middle, high], axis=0))
+    fill_edges(get, rims, put_rim)
+
+
+def fill_edges(get, rims, put_rim):
     for plane, dz in enumerate((-1, 1)):
         z = SIDE - 1 if dz < 0 else 0
         for px in range(SIDE + 2):
@@ -190,6 +194,126 @@
     return shifted_sum(blocks, down, up)
 
 
+def pieces_of(v, wide):
+    high = v.astype(BF16)
+    return (high, (v - high.astype(F32)).astype(BF16)) if wide else (high,)
+
+
+def multiplied(lhs, wide, matrix, blocks):
+    rows = [matrix.at[pl.ds(128 * at, 128)] for at in blocks]
+    take = lambda cols: jnp.concatenate([r[:, cols] for r in rows], axis=0)
+    cut = lambda v, at: v[:, 128 * at : 128 * at + 128]
+    if not wide:
+        sums = dot(lhs[0], take(slice(0, 384)))
+        return [cut(sums, k) for k in range(3)]
+    tops, rests = dot(lhs[0], take(slice(0, 768))), dot(lhs[1], take(slice(0, 384)))
+    return [cut(tops, k) + cut(tops, 3 + k) + cut(rests, k) for k in range(3)]
+
+
+def line_sum(blocks, down, up):
+    rows = blocks[0].shape[0]
+    down[8 : rows + 8] = blocks[0]
+    up[8 : rows + 8] = blocks[2]
+    zeros = jnp.zeros((SIDE, 128), F32)
+    for at in range(0, rows, 64):
+        down[pl.ds(7 + at, SIDE, stride=8)] = zeros
+        up[pl.ds(16 + at, SIDE, stride=8)] = zeros
+    return down[7 : rows + 7] + blocks[1] + up[9 : rows + 9]
+
+
+def clear_center(even, odd, wide):
+    for part in range(2 if wide else 1):
+        for px in (0, SIDE + 1):
+            even[part, px] = jnp.zeros(even.shape[2:], BF16)
+            odd[part, px] = jnp.zeros(odd.shape[2:], BF16)
+
+
+def fill_center(brick, wide, even, odd):
+    zeros = jnp.zeros((SIDE, 128), F32)
+    for x in range(SIDE):
+        middle = brick[64 * x : 64 * x + 64]
+        for part, v in enumerate(pieces_of(jnp.concatenate([zeros, middle, zeros], axis=0), wide)):
+            even[part, x + 1] = v
+        for part, v in enumerate(pieces_of(middle, wide)):
+            odd[part, x + 1] = v
+
+
+def center(wide, even, odd, down, up, matrix, first, last):
+    def taps(part):
+        windows = []
+        for i in range(3):
+            for j in range(3):
+                xs = slice(first + i, last + i)
+                v = odd[part, xs] if j == 1 else even[part, xs, 8 * j : 8 * j + 64]
+                windows.append(v.reshape((last - first) * 64, 128))
+        return jnp.concatenate(windows, axis=1)
+
+    lhs = [taps(part) for part in range(2 if wide else 1)]
+    return line_sum(multiplied(lhs, wide, matrix, range(9)), down, up)
+
+
+def fill_rims(load, link, wide, at, faces_even, faces_odd, edge, rims):
+    found = {o: link(o) for o in columns}
+    zeros = jnp.zeros((SIDE, 128), F32)
+
+    def get(o, start, size=SIDE, stride=1):
+        row, keep = found[o]
+        return load(row, start, size, stride) * keep
+
+    def put_face(face, lines):
+        v = jnp.concatenate(lines, axis=0)
+        for part, value in enumerate(pieces_of(v, wide)):
+            faces_even[part, face, at] = value
+        for part, value in enumerate(pieces_of(v[8:72], wide)):
+            faces_odd[part, face, at] = value
+
+    def put_rim(j, px, v):
+        for part, value in enumerate(pieces_of(v, wide)):
+            edge[part, j, at, px] = value
+
+    for face, d in enumerate((-1, 1)):
+        spot = SIDE - 1 if d < 0 else 0
+        put_face(face, [get((d, -1, 0), 64 * spot + 56), get((d, 0, 0), 64 * spot, 64), get((d, 1, 0), 64 * spot)])
+        lines = [get((0, d, 0), 64 * x + 8 * spot) for x in range(SIDE)]
+        put_face(2 + face, [zeros] + lines + [zeros])
+    fill_edges(get, rims, put_rim)
+
+
+def add_rims(sums, n, wide, faces_even, faces_odd, edge, down, up, matrix):
+    parts = range(2 if wide else 1)
+    for face in range(4):
+        side = 2 * (face % 2)
+        blocks = [3 * side + t for t in range(3)] if face < 2 else [3 * t + side for t in range(3)]
+        lhs = []
+        for part in parts:
+            windows = []
+            for t in range(3):
+                v = faces_odd[part, face] if t == 1 else faces_even[part, face, :, 8 * t : 8 * t + 64]
+                windows.append(v.reshape(n * 64, 128))
+            lhs.append(jnp.concatenate(windows, axis=1))
+        total = line_sum(multiplied(lhs, wide, matrix, blocks), down, up)
+        for b in range(n):
+            if face < 2:
+                sums[b, 224 * side : 224 * side + 64] += total[64 * b : 64 * b + 64]
+            else:
+                for x in range(SIDE):
+                    at = 64 * x + 28 * side
+                    sums[b, at : at + 8] += total[64 * b + 8 * x : 64 * b + 8 * x + 8]
+    lhs = []
+    for part in parts:
+        windows = [edge[part, j, :, i : i + 8].reshape(n * 128, 128) for i in range(3) for j in range(3)]
+        lhs.append(jnp.concatenate(windows, axis=1))
+    ends = lambda at: jnp.concatenate([matrix[:, at : at + 128], matrix[:, at + 256 : at + 384]], axis=1)
+    total = dot(lhs[0], ends(0))
+    if wide:
+        total = total + dot(lhs[0], ends(384)) + dot(lhs[1], ends(0))
+    for b in range(n):
+        for x in range(SIDE):
+            at = 128 * b + 16 * x
+            sums[b, pl.ds(64 * x, SIDE, stride=8)] += total[at : at + 8, 0:128]
+            sums[b, pl.ds(64 * x + 7, SIDE, stride=8)] += total[at + 8 : at + 16, 128:256]
+
+
 def surface_spots():
     spots = [(0, 0, 64, 1), (64, 448, 64, 1)]
     for x in range(1, 7):
@@ -273,6 +397,7 @@
     x, in_weight, one_weight, two_weight, out_weight, loads,
     matrix, last_matrix, one_matrix, two_matrix,
     even, odd, edge, wide_even, wide_odd, wide_edge, rims, shift_down, shift_up,
+    faces_even, faces_odd, face_edge, wide_faces_even, wide_faces_odd, wide_face_edge, wide_sums,
     parts, turned, hidden, halves, small, grown,
     x_send, x_halo, hidden_send, hidden_halo,
     code_block, codes, code_table, table, code_scalars, table_scalars,
@@ -403,6 +528,15 @@
     for pair in range(pairs):
         for one, v in enumerate(doubled(turned[pair])):
             parts[HALO + 2 * pair + one] = parted(v)
+
+    clear_center(even, odd, False)
+
+    def own_step(i, carry):
+        fill_center(parts.at[HALO + i], False, even, odd)
+        hidden[i] = center(False, even, odd, shift_down, shift_up, matrix, 0, SIDE)
+        return carry
+
+    lax.fori_loop(0, count, own_step, 0)
     end_shared(code_block, code_at, send_codes, recv_codes)
     lane = lax.broadcasted_iota(jnp.int32, (SIDE, 128), 1)
     table_rows = jnp.full((SIDE, 128), -1, jnp.int32)
@@ -439,7 +573,7 @@
     end_halo(x_copies)
     for side, at in ((0, 0), (1, HALO + count)):
         unpack_pair(x_halo[side], halves, parts.at[at], parts.at[at + 1])
-    fine_scratch = (even, odd, edge, rims, shift_down, shift_up)
+    fine_scratch = (even.at[0], odd.at[0], edge, rims, shift_down, shift_up)
     two = lambda bias: jnp.concatenate([bias[...], bias[...]], axis=1)
     in_both = two(in_bias)
 
@@ -449,8 +583,19 @@
     def pooled_copies(i):
         return shared_copies(pooled.at[members + member, i], pooled_at(i), send_pooled.at[i], recv_pooled.at[i])
 
+    def rim_step(i, carry):
+        fill_rims(
+            loader(parts, HALO + i), linker(fine_links, i, fine_start, HALO + i, parts.shape[0]), False, i,
+            faces_even, faces_odd, face_edge, rims,
+        )
+        return carry
+
+    lax.fori_loop(0, count, rim_step, 0)
+    add_rims(hidden, count, False, faces_even, faces_odd, face_edge, shift_down, shift_up, matrix)
+
     def first_step(i, carry):
-        v = silu(fine_conv(parts, HALO + i, fine_start, fine_links, i, fine_scratch, matrix) + in_both)
+        v = hidden[i]
+        v = silu(v + pltpu.roll(v, 64, 1) + in_both)
         pool(v, small, pooled.at[members + member, i])
         hidden[i] = v
         start_shared(pooled_copies(i))
@@ -517,11 +662,16 @@
             for c in range(len(CHUNKS)):
                 direct(i, c).start()
 
-        def end_first():
-            for i in range(slots):
-                for c in range(len(CHUNKS)):
-                    came(i, c).wait_recv()
-                    pl.when(relays_out)(relay(i, c).start)
+        arrivals = [(i, c) for i in range(slots) for c in range(len(CHUNKS))]
+
+        def pass_on(at):
+            i, c = arrivals[at]
+            came(i, c).wait_recv()
+            pl.when(relays_out)(relay(i, c).start)
+
+        def end_first(passed):
+            for at in range(passed, len(arrivals)):
+                pass_on(at)
             for i in range(slots):
                 for c in range(len(CHUNKS)):
                     pl.when(relays_in)(relay(i, c).wait_recv)
@@ -541,7 +691,10 @@
         def start_first(i):
             start_halo(sides(i))
 
-        def end_first():
+        def pass_on(at):
+            pass
+
+        def end_first(passed):
             for i in range(slots):
                 end_halo(sides(i))
 
@@ -561,13 +714,36 @@
     up_high = high_of(turned_up)
     up_both = jnp.concatenate([up_high, turned_up - up_high], axis=1)
     up_matrix = jnp.concatenate([up_both, up_both], axis=0).astype(BF16)
-    end_first()
+    clear_center(wide_even, wide_odd, True)
+    passed = 0
+    for i in range(slots):
+        fill_center(first.at[slots + i], True, wide_even, wide_odd)
+        for half in range(2):
+            pass_on(passed)
+            passed += 1
+            spot = slice(256 * half, 256 * half + 256)
+            wide_sums[i, spot] = center(
+                True, wide_even, wide_odd, shift_down, shift_up, two_matrix, 4 * half, 4 * half + 4
+            )
+    end_first(passed)
     for side, at in ((0, 0), (1, 2 * slots)):
         for i in range(slots):
             unpack(first_halo.at[side, i], first.at[at + i])
 
+    def wide_rim_step(i, carry):
+        fill_rims(
+            loader(first, slots + i), linker(coarse_links, i, coarse_start, slots + i, first.shape[0]), True, i,
+            wide_faces_even, wide_faces_odd, wide_face_edge, rims,
+        )
+        return carry
+
+    lax.fori_loop(0, slots, wide_rim_step, 0)
+    add_rims(
+        wide_sums, slots, True, wide_faces_even, wide_faces_odd, wide_face_edge, shift_down, shift_up, two_matrix
+    )
+
     def third_step(i, carry):
-        v = silu(coarse_conv(first, slots + i, coarse_start, coarse_links, i, wide_scratch, two_matrix) + two_bias[...])
+        v = silu(wide_sums[i] + two_bias[...])
         high = v.astype(BF16)
         low = (v - high.astype(F32)).astype(BF16)
         sums = dot(jnp.concatenate([high, low], axis=1), up_matrix)
@@ -711,9 +887,12 @@
         floats(*x.shape), floats(*in_weight.shape), floats(*one_weight.shape), floats(*two_weight.shape),
         floats(*out_weight.shape), sems(5),
         halfs(1152, 384), halfs(1152, 384), halfs(1152, 768), halfs(1152, 768),
-        halfs(10, 80, 128), halfs(10, 64, 128), halfs(3, 10, 16, 128),
+        halfs(1, 10, 80, 128), halfs(1, 10, 64, 128), halfs(3, 10, 16, 128),
         halfs(2, 10, 80, 128), halfs(2, 10, 64, 128), halfs(2, 3, 10, 16, 128),
         floats(2, 10 * LINE, 128), floats(VOX + 16, 128), floats(VOX + 16, 128),
+        halfs(1, 4, count, 80, 128), halfs(1, 4, count, 64, 128), halfs(1, 3, count, 10, 16, 128),
+        halfs(2, 4, slots, 80, 128), halfs(2, 4, slots, 64, 128), halfs(2, 3, slots, 10, 16, 128),
+        floats(slots, VOX, 128),
         floats(span, VOX, 128), floats(count // 2, VOX, 128), floats(count, VOX, 128),
         floats(2, SURFACE, 128), floats(128, 128), floats(HALO, VOX, 128),
         floats(2, SURFACE, 128), floats(2, SURFACE, 128), floats(2, SURFACE, 128), floats(2, SURFACE, 128),

time: 63.5 us -> 61.2 us (0.964)
  Pallas kernels: 61 us -> 59.1 us
    pallas_call x1, Pallas kernels: 61 us -> 59.1 us  [per_device(): pl.pallas_call(step_kernel, out_shape=jax.ShapeDtypeStruct(x.shape, F32),...]
where the time goes in v3:
time: 61.2 us; the launch traced here: 61 us
  Pallas kernels  59.1 us (97%)
  local copies, waits for them, and re-layouts  1.87 us (3%)
    pallas_call x1, Pallas kernels, per_device(): pl.pallas_call(step_kernel, out_shape=jax.ShapeDtypeStruct(x.shape, F32),...  59.1 us
    unnamed x1, local copies, waits for them, and re-layouts  1.87 us

profile of v3, /device:TPU:0, one launch (start us, length us, event | category | flops | bytes accessed | tf_op | source)
XLA Modules:
  0.0 61.0 jit_solution(16815695821630319414)
XLA Ops:
  0.0 59.1 %step.1 = f32[4,64,512]{2,1,0:T(8,128)} custom-call(f32[4,64,512]{2,1,0:T(8,128)} %x_any.1, s32[4,26]{1,0:T(4,128)} %fine_links.1, s32[4]{0:T(128)} %own_codes.1, s32[2,26]{1,0:T(2,128)} %coarse_links.1, f32[64,1728]{1,0:T(8,128)} %in_any.1, f32[1,64]{1,0:T(1,128)} %bitcast.6, f32[64,128]{1,0:T(8,128)} %bitcast.5, f32[128,3456]{1,0:T(8,128)} %one_any.1, ...), custom_call_target="tpu_custom_call" | custom-call | tf_op jit(solution)/shard_map/step/pallas_call | solution.py:909
  59.1 1.9 %copy.16 = f32[4,64,512]{2,1,0:T(8,128)} copy(f32[4,64,512]{2,1,0:T(8,128)} %step.1) | data formatting | bytes 1048576

commit v4 on v3

--- a/solution.py
+++ b/solution.py
@@ -92,24 +92,23 @@
 
 
 def stacked(even, odd, edge):
-    taps = []
+    mains, rims = [], []
     for i in range(3):
         for j in range(3):
             main = odd[i : i + 8] if j == 1 else even[i : i + 8, 8 * j : 8 * j + 64]
-            rim = edge[j, i : i + 8]
-            taps.append(jnp.concatenate([main.reshape(VOX, 128), rim.reshape(128, 128)], axis=0))
-    return jnp.concatenate(taps, axis=1)
-
-
-def shifted_sum(blocks, down, up):
+            mains.append(main.reshape(VOX, 128))
+            rims.append(edge[j, i : i + 8].reshape(128, 128))
+    return jnp.concatenate(mains, axis=1), jnp.concatenate(rims, axis=1)
+
+
+def shifted_sum(blocks, edges, down, up):
     before, here, after = blocks
-    down[8 : VOX + 8] = before[:VOX]
-    up[8 : VOX + 8] = after[:VOX]
+    down[8 : VOX + 8] = before
+    up[8 : VOX + 8] = after
     for x in range(SIDE):
-        rim = VOX + 16 * x
-        down[pl.ds(7 + 64 * x, SIDE, stride=8)] = before[rim : rim + 8]
-        up[pl.ds(16 + 64 * x, SIDE, stride=8)] = after[rim + 8 : rim + 16]
-    return down[7 : VOX + 7] + here[:VOX] + up[9 : VOX + 9]
+        down[pl.ds(7 + 64 * x, SIDE, stride=8)] = edges[16 * x : 16 * x + 8, 0:128]
+        up[pl.ds(16 + 64 * x, SIDE, stride=8)] = edges[16 * x + 8 : 16 * x + 16, 128:256]
+    return down[7 : VOX + 7] + here + up[9 : VOX + 9]
 
 
 def fine_matrix(weight, matrix):
@@ -163,8 +162,11 @@
         edge[j, px] = v.astype(BF16)
 
     fill(loader(parts, own), linker(links, brick, start, own, parts.shape[0]), put, rims, put_rim)
-    sums = dot(stacked(even, odd, edge), matrix[...])
-    out = shifted_sum([sums[:, 128 * k : 128 * k + 128] for k in range(3)], down, up)
+    main, rim = stacked(even, odd, edge)
+    sums = dot(main, matrix[...])
+    ends = lambda at: jnp.concatenate([matrix[:, at : at + 128], matrix[:, at + 256 : at + 384]], axis=1)
+    edges = dot(rim, ends(0))
+    out = shifted_sum([sums[:, 128 * k : 128 * k + 128] for k in range(3)], edges, down, up)
     return out + pltpu.roll(out, 64, 1)
 
 
@@ -187,11 +189,14 @@
         edge[1, j, px] = (v - high.astype(F32)).astype(BF16)
 
     fill(loader(parts, own), linker(links, brick, start, own, parts.shape[0]), put, rims, put_rim)
-    tops = dot(stacked(even.at[0], odd.at[0], edge.at[0]), matrix[...])
-    rests = dot(stacked(even.at[1], odd.at[1], edge.at[1]), matrix[:, 0:384])
+    (main_0, rim_0), (main_1, rim_1) = (stacked(even.at[p], odd.at[p], edge.at[p]) for p in range(2))
+    tops = dot(main_0, matrix[...])
+    rests = dot(main_1, matrix[:, 0:384])
+    ends = lambda at: jnp.concatenate([matrix[:, at : at + 128], matrix[:, at + 256 : at + 384]], axis=1)
+    edges = dot(rim_0, ends(0)) + dot(rim_0, ends(384)) + dot(rim_1, ends(0))
     cut = lambda v, at: v[:, 128 * at : 128 * at + 128]
     blocks = [cut(tops, k) + cut(tops, 3 + k) + cut(rests, k) for k in range(3)]
-    return shifted_sum(blocks, down, up)
+    return shifted_sum(blocks, edges, down, up)
 
 
 def pieces_of(v, wide):
@@ -500,10 +505,12 @@
         pl.when(has_high)(to_high.start)
         pl.when(has_low)(to_low.start)
 
-    def end_shared(source, at, send, recv):
+    def end_near(source, at, send, recv):
         for k in range(1, members):
             other = (member + k) % members
             remote(source, at(members + other), send.at[k], recv.at[members + other], (group, other)).wait_recv()
+
+    def end_far(source, at, send, recv):
         for k in range(members):
             from_low = remote(source, at(k), send.at[0], recv.at[k], low_at)
             from_high = remote(source, at(2 * members + k), send.at[0], recv.at[2 * members + k], high_at)
@@ -537,7 +544,8 @@
         return carry
 
     lax.fori_loop(0, count, own_step, 0)
-    end_shared(code_block, code_at, send_codes, recv_codes)
+    end_near(code_block, code_at, send_codes, recv_codes)
+    end_far(code_block, code_at, send_codes, recv_codes)
     lane = lax.broadcasted_iota(jnp.int32, (SIDE, 128), 1)
     table_rows = jnp.full((SIDE, 128), -1, jnp.int32)
     for near in range(3):
@@ -560,6 +568,44 @@
     to_codes = pltpu.make_async_copy(code_table, code_scalars, local_sems.at[1])
     to_table.start()
     to_codes.start()
+
+    fine_start = position * count - HALO
+    end_halo(x_copies)
+    for side, at in ((0, 0), (1, HALO + count)):
+        unpack_pair(x_halo[side], halves, parts.at[at], parts.at[at + 1])
+    fine_scratch = (even.at[0], odd.at[0], edge, rims, shift_down, shift_up)
+    two = lambda bias: jnp.concatenate([bias[...], bias[...]], axis=1)
+    in_both = two(in_bias)
+
+    def pooled_at(i):
+        return lambda k: pooled.at[k, i]
+
+    def pooled_copies(i):
+        return shared_copies(pooled.at[members + member, i], pooled_at(i), send_pooled.at[i], recv_pooled.at[i])
+
+    def rim_step(i, carry):
+        fill_rims(
+            loader(parts, HALO + i), linker(fine_links, i, fine_start, HALO + i, parts.shape[0]), False, i,
+            faces_even, faces_odd, face_edge, rims,
+        )
+        return carry
+
+    lax.fori_loop(0, count, rim_step, 0)
+    add_rims(hidden, count, False, faces_even, faces_odd, face_edge, shift_down, shift_up, matrix)
+
+    def first_step(i, carry):
+        v = hidden[i]
+        v = silu(v + pltpu.roll(v, 64, 1) + in_both)
+        pool(v, small, pooled.at[members + member, i])
+        hidden[i] = v
+        start_shared(pooled_copies(i))
+        return carry
+
+    lax.fori_loop(0, count, first_step, 0)
+    pack(lambda spot: merged(hidden[0, spot], hidden[1, spot]), hidden_send.at[0])
+    pack(lambda spot: merged(hidden[count - 2, spot], hidden[count - 1, spot]), hidden_send.at[1])
+    hidden_copies = halo_copies(hidden_send, hidden_halo, send_hidden, recv_hidden)
+    pl.when(has_left)(hidden_copies[0].start)
     fetches[2].wait()
     coarse_matrix(one_weight, one_matrix)
     fetches[3].wait()
@@ -569,63 +615,33 @@
     to_table.wait()
     to_codes.wait()
 
-    fine_start = position * count - HALO
-    end_halo(x_copies)
-    for side, at in ((0, 0), (1, HALO + count)):
-        unpack_pair(x_halo[side], halves, parts.at[at], parts.at[at + 1])
-    fine_scratch = (even.at[0], odd.at[0], edge, rims, shift_down, shift_up)
-    two = lambda bias: jnp.concatenate([bias[...], bias[...]], axis=1)
-    in_both = two(in_bias)
-
-    def pooled_at(i):
-        return lambda k: pooled.at[k, i]
-
-    def pooled_copies(i):
-        return shared_copies(pooled.at[members + member, i], pooled_at(i), send_pooled.at[i], recv_pooled.at[i])
-
-    def rim_step(i, carry):
-        fill_rims(
-            loader(parts, HALO + i), linker(fine_links, i, fine_start, HALO + i, parts.shape[0]), False, i,
-            faces_even, faces_odd, face_edge, rims,
-        )
-        return carry
-
-    lax.fori_loop(0, count, rim_step, 0)
-    add_rims(hidden, count, False, faces_even, faces_odd, face_edge, shift_down, shift_up, matrix)
-
-    def first_step(i, carry):
-        v = hidden[i]
-        v = silu(v + pltpu.roll(v, 64, 1) + in_both)
-        pool(v, small, pooled.at[members + member, i])
-        hidden[i] = v
-        start_shared(pooled_copies(i))
-        return carry
-
-    lax.fori_loop(0, count, first_step, 0)
-    pack(lambda spot: merged(hidden[0, spot], hidden[1, spot]), hidden_send.at[0])
-    pack(lambda spot: merged(hidden[count - 2, spot], hidden[count - 1, spot]), hidden_send.at[1])
-    hidden_copies = halo_copies(hidden_send, hidden_halo, send_hidden, recv_hidden)
-    start_halo(hidden_copies)
-
     turned_down = down_weight[...]
     down_high = high_of(turned_down)
     down_both = jnp.concatenate([down_high, turned_down - down_high], axis=1)
     down_matrix = jnp.concatenate([down_both, down_both], axis=0).astype(BF16)
     for i in range(count):
-        end_shared(pooled.at[members + member, i], pooled_at(i), send_pooled.at[i], recv_pooled.at[i])
-
-    def base_step(slot, carry):
-        for octant in range(8):
-            which = table_scalars[slot // slots, slot % slots * 8 + octant]
-            there_is = which >= 0
-            which = jnp.where(there_is, jnp.minimum(which, 3 * members * count - 1), (members + member) * count)
-            keep = jnp.where(there_is, 1.0, 0.0).astype(F32)
-            place_piece(pooled[which // count, which % count] * keep, octant, placed)
-        sums = dot(placed[...].astype(BF16), down_matrix)
-        base[slot] = swap_halves(sums[:, 0:128] + sums[:, 128:256], True)
+        end_near(pooled.at[members + member, i], pooled_at(i), send_pooled.at[i], recv_pooled.at[i])
+    for i in range(count):
+        end_far(pooled.at[members + member, i], pooled_at(i), send_pooled.at[i], recv_pooled.at[i])
+
+    def base_of(near):
+        for slot in range(slots):
+            for octant in range(8):
+                which = table_scalars[near, slot * 8 + octant]
+                there_is = which >= 0
+                which = jnp.where(there_is, jnp.minimum(which, 3 * members * count - 1), (members + member) * count)
+                keep = jnp.where(there_is, 1.0, 0.0).astype(F32)
+                place_piece(pooled[which // count, which % count] * keep, octant, placed.at[slot])
+        sums = dot(placed[...].reshape(slots * VOX, 128).astype(BF16), down_matrix)
+        sums = sums[:, 0:128] + sums[:, 128:256]
+        for slot in range(slots):
+            base[near * slots + slot] = swap_halves(sums[slot * VOX : slot * VOX + VOX], True)
+
+    def base_step(t, carry):
+        base_of(t)
         return carry
 
-    lax.fori_loop(0, 3 * slots, base_step, 0)
+    lax.fori_loop(0, 3, base_step, 0)
     coarse_start = (position - 1) * slots
     wide_scratch = (wide_even, wide_odd, wide_edge, rims, shift_down, shift_up)
 
@@ -710,6 +726,7 @@
         return carry
 
     lax.fori_loop(0, slots, second_step, 0)
+    pl.when(has_right)(hidden_copies[1].start)
     turned_up = up_weight[...].T
     up_high = high_of(turned_up)
     up_both = jnp.concatenate([up_high, turned_up - up_high], axis=1)
@@ -747,8 +764,8 @@
         high = v.astype(BF16)
         low = (v - high.astype(F32)).astype(BF16)
         sums = dot(jnp.concatenate([high, low], axis=1), up_matrix)
-        placed[...] = swap_halves(sums + pltpu.roll(sums, 64, 1), False)
-        take_pieces(placed, lifted.at[pl.ds(i * 8, 8)])
+        placed[0] = swap_halves(sums + pltpu.roll(sums, 64, 1), False)
+        take_pieces(placed.at[0], lifted.at[pl.ds(i * 8, 8)])
         return carry
 
     lax.fori_loop(0, slots, third_step, 0)
@@ -898,7 +915,7 @@
         floats(2, SURFACE, 128), floats(2, SURFACE, 128), floats(2, SURFACE, 128), floats(2, SURFACE, 128),
         ints(8, 128), ints(3 * members, 8, 128), ints(members, 8, 128), ints(8, 128),
         pltpu.SMEM((members, 8, 128), jnp.int32), pltpu.SMEM((8, 128), jnp.int32),
-        floats(3 * members, count, *wire), floats(VOX, 128), floats(3 * slots, VOX, 128), floats(3 * slots, VOX, 128),
+        floats(3 * members, count, *wire), floats(slots, VOX, 128), floats(3 * slots, VOX, 128), floats(3 * slots, VOX, 128),
         floats(slots, SURFACE, 128), floats(2, slots, SURFACE, 128), floats(slots * 8, *wire),
         floats(members * count + 2 * HALO, *wire), floats(members, span, *wire), floats(members, HALO, *wire),
         floats(members, HALO, *wire),

time: 61.2 us -> 59.4 us (0.971)
  Pallas kernels: 59.1 us -> 57.2 us
    pallas_call x1, Pallas kernels: 59.1 us -> 57.2 us  [per_device(): pl.pallas_call(step_kernel, out_shape=jax.ShapeDtypeStruct(x.shape, F32),...]
where the time goes in v4:
time: 59.4 us; the launch traced here: 59.1 us
  Pallas kernels  57.2 us (96%)
  local copies, waits for them, and re-layouts  1.87 us (3%)
    pallas_call x1, Pallas kernels, per_device(): pl.pallas_call(step_kernel, out_shape=jax.ShapeDtypeStruct(x.shape, F32),...  57.2 us
    unnamed x1, local copies, waits for them, and re-layouts  1.87 us

profile of v4, /device:TPU:0, one launch (start us, length us, event | category | flops | bytes accessed | tf_op | source)
XLA Modules:
  0.0 59.1 jit_solution(11562337945062144709)
XLA Ops:
  0.0 57.2 %step.1 = f32[4,64,512]{2,1,0:T(8,128)} custom-call(f32[4,64,512]{2,1,0:T(8,128)} %x_any.1, s32[4,26]{1,0:T(4,128)} %fine_links.1, s32[4]{0:T(128)} %own_codes.1, s32[2,26]{1,0:T(2,128)} %coarse_links.1, f32[64,1728]{1,0:T(8,128)} %in_any.1, f32[1,64]{1,0:T(1,128)} %bitcast.6, f32[64,128]{1,0:T(8,128)} %bitcast.5, f32[128,3456]{1,0:T(8,128)} %one_any.1, ...), custom_call_target="tpu_custom_call" | custom-call | tf_op jit(solution)/shard_map/step/pallas_call | solution.py:926
  57.2 1.9 %copy.16 = f32[4,64,512]{2,1,0:T(8,128)} copy(f32[4,64,512]{2,1,0:T(8,128)} %step.1) | data formatting | bytes 1048576

commit v5 on v4

--- a/solution.py
+++ b/solution.py
@@ -16,6 +16,7 @@
 SURFACE = VOX - 6 * 6 * 6
 LINE = 24
 LIMIT = 62 * 1024 * 1024
+EARLY = 160
 CHUNKS = ((0, 96), (96, 96), (192, 104))
 
 offsets = [(x, y, z) for x in (-1, 0, 1) for y in (-1, 0, 1) for z in (-1, 0, 1)]
@@ -472,9 +473,10 @@
         + jnp.where(has_low, 1, 0) + jnp.where(has_high, 1, 0),
     )
 
-    def halo_copies(source, halo, send, recv):
-        to_left = remote(source.at[0], halo.at[1], send.at[0], recv.at[1], left_at)
-        to_right = remote(source.at[1], halo.at[0], send.at[1], recv.at[0], right_at)
+    def halo_copies(source, halo, send, recv, at=0, rows=SURFACE):
+        spot = pl.ds(at, rows)
+        to_left = remote(source.at[0, spot], halo.at[1, spot], send.at[0], recv.at[1], left_at)
+        to_right = remote(source.at[1, spot], halo.at[0, spot], send.at[1], recv.at[0], right_at)
         return to_left, to_right
 
     def start_halo(copies):
@@ -583,29 +585,32 @@
     def pooled_copies(i):
         return shared_copies(pooled.at[members + member, i], pooled_at(i), send_pooled.at[i], recv_pooled.at[i])
 
-    def rim_step(i, carry):
-        fill_rims(
-            loader(parts, HALO + i), linker(fine_links, i, fine_start, HALO + i, parts.shape[0]), False, i,
-            faces_even, faces_odd, face_edge, rims,
-        )
+    def first_step(pair, carry):
+        at = 2 * pair
+        for one in range(2):
+            own = HALO + at + one
+            fill_rims(
+                loader(parts, own), linker(fine_links, at + one, fine_start, own, parts.shape[0]), False, one,
+                faces_even, faces_odd, face_edge, rims,
+            )
+        sums = hidden.at[pl.ds(at, 2)]
+        add_rims(sums, 2, False, faces_even, faces_odd, face_edge, shift_down, shift_up, matrix)
+        for one in range(2):
+            v = sums[one]
+            v = silu(v + pltpu.roll(v, 64, 1) + in_both)
+            pool(v, small, pooled.at[members + member, at + one])
+            sums[one] = v
+            start_shared(pooled_copies(at + one))
         return carry
 
-    lax.fori_loop(0, count, rim_step, 0)
-    add_rims(hidden, count, False, faces_even, faces_odd, face_edge, shift_down, shift_up, matrix)
-
-    def first_step(i, carry):
-        v = hidden[i]
-        v = silu(v + pltpu.roll(v, 64, 1) + in_both)
-        pool(v, small, pooled.at[members + member, i])
-        hidden[i] = v
-        start_shared(pooled_copies(i))
-        return carry
-
-    lax.fori_loop(0, count, first_step, 0)
+    lax.fori_loop(0, pairs, first_step, 0)
     pack(lambda spot: merged(hidden[0, spot], hidden[1, spot]), hidden_send.at[0])
     pack(lambda spot: merged(hidden[count - 2, spot], hidden[count - 1, spot]), hidden_send.at[1])
-    hidden_copies = halo_copies(hidden_send, hidden_halo, send_hidden, recv_hidden)
-    pl.when(has_left)(hidden_copies[0].start)
+    hidden_copies = [
+        halo_copies(hidden_send, hidden_halo, send_hidden.at[part], recv_hidden.at[part], at, rows)
+        for part, (at, rows) in enumerate(((0, EARLY), (EARLY, SURFACE - EARLY)))
+    ]
+    start_halo(hidden_copies[0])
     fetches[2].wait()
     coarse_matrix(one_weight, one_matrix)
     fetches[3].wait()
@@ -726,7 +731,6 @@
         return carry
 
     lax.fori_loop(0, slots, second_step, 0)
-    pl.when(has_right)(hidden_copies[1].start)
     turned_up = up_weight[...].T
     up_high = high_of(turned_up)
     up_both = jnp.concatenate([up_high, turned_up - up_high], axis=1)
@@ -743,6 +747,7 @@
                 True, wide_even, wide_odd, shift_down, shift_up, two_matrix, 4 * half, 4 * half + 4
             )
     end_first(passed)
+    start_halo(hidden_copies[1])
     for side, at in ((0, 0), (1, 2 * slots)):
         for i in range(slots):
             unpack(first_halo.at[side, i], first.at[at + i])
@@ -822,7 +827,8 @@
     pl.when(has_high)(to_high.start)
     pl.when(has_low)(to_low.start)
     window[member] = wanted[pl.ds(member * count, count + 2 * HALO)]
-    end_halo(hidden_copies)
+    for copies in hidden_copies:
+        end_halo(copies)
     for k in range(1, members):
         from_member(k, 0).wait_recv()
 
@@ -873,7 +879,8 @@
     end_shared_sends(code_copies)
     for i in range(count):
         end_shared_sends(pooled_copies(i))
-    end_halo_sends(hidden_copies)
+    for copies in hidden_copies:
+        end_halo_sends(copies)
     end_first_sends()
     for k in range(1, members):
         to_member(k, 0).wait_send()
@@ -907,7 +914,7 @@
         halfs(1, 10, 80, 128), halfs(1, 10, 64, 128), halfs(3, 10, 16, 128),
         halfs(2, 10, 80, 128), halfs(2, 10, 64, 128), halfs(2, 3, 10, 16, 128),
         floats(2, 10 * LINE, 128), floats(VOX + 16, 128), floats(VOX + 16, 128),
-        halfs(1, 4, count, 80, 128), halfs(1, 4, count, 64, 128), halfs(1, 3, count, 10, 16, 128),
+        halfs(1, 4, 2, 80, 128), halfs(1, 4, 2, 64, 128), halfs(1, 3, 2, 10, 16, 128),
         halfs(2, 4, slots, 80, 128), halfs(2, 4, slots, 64, 128), halfs(2, 3, slots, 10, 16, 128),
         floats(slots, VOX, 128),
         floats(span, VOX, 128), floats(count // 2, VOX, 128), floats(count, VOX, 128),
@@ -919,7 +926,7 @@
         floats(slots, SURFACE, 128), floats(2, slots, SURFACE, 128), floats(slots * 8, *wire),
         floats(members * count + 2 * HALO, *wire), floats(members, span, *wire), floats(members, HALO, *wire),
         floats(members, HALO, *wire),
-        sems(2), sems(2), sems(2), sems(2), sems(2), sems(members + 1), sems(3 * members),
+        sems(2), sems(2), sems(2), sems(2, 2), sems(2, 2), sems(members + 1), sems(3 * members),
         sems(count, members + 1), sems(count, 3 * members),
         sems(slots, 3), sems(slots, 3), sems(slots, 3), sems(slots, 3), sems(members + 1, 3), sems(3 * members, 3),
     ]

time: 59.4 us -> 57.4 us (0.966)
  Pallas kernels: 57.2 us -> 55.3 us
    pallas_call x1, Pallas kernels: 57.2 us -> 55.3 us  [per_device(): pl.pallas_call(step_kernel, out_shape=jax.ShapeDtypeStruct(x.shape, F32),...]
where the time goes in v5:
time: 57.4 us; the launch traced here: 57.2 us
  Pallas kernels  55.3 us (96%)
  local copies, waits for them, and re-layouts  1.87 us (3%)
    pallas_call x1, Pallas kernels, per_device(): pl.pallas_call(step_kernel, out_shape=jax.ShapeDtypeStruct(x.shape, F32),...  55.3 us
    unnamed x1, local copies, waits for them, and re-layouts  1.87 us

profile of v5, /device:TPU:0, one launch (start us, length us, event | category | flops | bytes accessed | tf_op | source)
XLA Modules:
  0.0 57.2 jit_solution(9807254976933206080)
XLA Ops:
  0.0 55.3 %step.1 = f32[4,64,512]{2,1,0:T(8,128)} custom-call(f32[4,64,512]{2,1,0:T(8,128)} %x_any.1, s32[4,26]{1,0:T(4,128)} %fine_links.1, s32[4]{0:T(128)} %own_codes.1, s32[2,26]{1,0:T(2,128)} %coarse_links.1, f32[64,1728]{1,0:T(8,128)} %in_any.1, f32[1,64]{1,0:T(1,128)} %bitcast.6, f32[64,128]{1,0:T(8,128)} %bitcast.5, f32[128,3456]{1,0:T(8,128)} %one_any.1, ...), custom_call_target="tpu_custom_call" | custom-call | tf_op jit(solution)/shard_map/step/pallas_call | solution.py:933
  55.3 1.9 %copy.16 = f32[4,64,512]{2,1,0:T(8,128)} copy(f32[4,64,512]{2,1,0:T(8,128)} %step.1) | data formatting | bytes 1048576

commit v6 on v5

--- a/solution.py
+++ b/solution.py
@@ -17,7 +17,8 @@
 LINE = 24
 LIMIT = 62 * 1024 * 1024
 EARLY = 160
-CHUNKS = ((0, 96), (96, 96), (192, 104))
+CHUNKS = ((0, 120), (120, 96), (216, 80))
+STRAIGHT = 1
 
 offsets = [(x, y, z) for x in (-1, 0, 1) for y in (-1, 0, 1) for z in (-1, 0, 1)]
 columns = {o: k for k, o in enumerate(o for o in offsets if o != (0, 0, 0))}
@@ -679,16 +680,29 @@
                 send_relay.at[i, c], recv_relay.at[i, c], relay_at,
             )
 
+        exists = jnp.where(parity == 0, has_left, has_right)
+        far_at = tuple(jnp.where(parity == 0, a, b) for a, b in zip(left_at, right_at))
+
+        def far(i, c):
+            spot = pl.ds(*CHUNKS[c])
+            return remote(
+                first_send.at[i, spot], first_halo.at[1 - parity, i, spot],
+                send_relay.at[i, c], recv_relay.at[i, c], far_at,
+            )
+
         def start_first(i):
             for c in range(len(CHUNKS)):
                 direct(i, c).start()
+            for c in range(len(CHUNKS) - STRAIGHT, len(CHUNKS)):
+                pl.when((i == slots - 1) & exists)(far(i, c).start)
 
         arrivals = [(i, c) for i in range(slots) for c in range(len(CHUNKS))]
 
         def pass_on(at):
             i, c = arrivals[at]
             came(i, c).wait_recv()
-            pl.when(relays_out)(relay(i, c).start)
+            if at < len(arrivals) - STRAIGHT:
+                pl.when(relays_out)(relay(i, c).start)
 
         def end_first(passed):
             for at in range(passed, len(arrivals)):
@@ -698,10 +712,12 @@
                     pl.when(relays_in)(relay(i, c).wait_recv)
 
         def end_first_sends():
-            for i in range(slots):
-                for c in range(len(CHUNKS)):
-                    direct(i, c).wait_send()
+            for at, (i, c) in enumerate(arrivals):
+                direct(i, c).wait_send()
+                if at < len(arrivals) - STRAIGHT:
                     pl.when(relays_out)(relay(i, c).wait_send)
+                else:
+                    pl.when(exists)(far(i, c).wait_send)
     else:
 
         def sides(i):

time: 57.4 us -> 56.7 us (0.988)
  Pallas kernels: 55.3 us -> 54.5 us
    pallas_call x1, Pallas kernels: 55.3 us -> 54.5 us  [per_device(): pl.pallas_call(step_kernel, out_shape=jax.ShapeDtypeStruct(x.shape, F32),...]
where the time goes in v6:
time: 56.7 us; the launch traced here: 56.4 us
  Pallas kernels  54.5 us (96%)
  local copies, waits for them, and re-layouts  1.87 us (3%)
    pallas_call x1, Pallas kernels, per_device(): pl.pallas_call(step_kernel, out_shape=jax.ShapeDtypeStruct(x.shape, F32),...  54.5 us
    unnamed x1, local copies, waits for them, and re-layouts  1.87 us

profile of v6, /device:TPU:0, one launch (start us, length us, event | category | flops | bytes accessed | tf_op | source)
XLA Modules:
  0.0 56.4 jit_solution(551415591871840506)
XLA Ops:
  0.0 54.5 %step.1 = f32[4,64,512]{2,1,0:T(8,128)} custom-call(f32[4,64,512]{2,1,0:T(8,128)} %x_any.1, s32[4,26]{1,0:T(4,128)} %fine_links.1, s32[4]{0:T(128)} %own_codes.1, s32[2,26]{1,0:T(2,128)} %coarse_links.1, f32[64,1728]{1,0:T(8,128)} %in_any.1, f32[1,64]{1,0:T(1,128)} %bitcast.6, f32[64,128]{1,0:T(8,128)} %bitcast.5, f32[128,3456]{1,0:T(8,128)} %one_any.1, ...), custom_call_target="tpu_custom_call" | custom-call | tf_op jit(solution)/shard_map/step/pallas_call | solution.py:949
  54.5 1.9 %copy.16 = f32[4,64,512]{2,1,0:T(8,128)} copy(f32[4,64,512]{2,1,0:T(8,128)} %step.1) | data formatting | bytes 1048576

commit v7 on v6

--- a/solution.py
+++ b/solution.py
@@ -170,6 +170,59 @@
     edges = dot(rim, ends(0))
     out = shifted_sum([sums[:, 128 * k : 128 * k + 128] for k in range(3)], edges, down, up)
     return out + pltpu.roll(out, 64, 1)
+
+
+def packed_matrix(weight, matrix):
+    w = weight[...]
+    for ij in range(9):
+        ks = [w[:, 64 * (3 * ij + k) : 64 * (3 * ij + k) + 64] for k in (0, 1, 2, 2)]
+        block = jnp.concatenate(ks, axis=0).T
+        high = high_of(block)
+        low = (block - high).astype(BF16)
+        high = high.astype(BF16)
+        matrix[128 * ij : 128 * ij + 64] = high
+        matrix[128 * ij + 64 : 128 * ij + 128] = high
+        i, j = ij // 3, ij % 3
+        at = 1152 + 128 * j + 64 * i if i < 2 else (1536, 1664, 1600)[j]
+        matrix[at : at + 64] = low
+    matrix[1728:1792] = jnp.zeros((64, 256), BF16)
+
+
+def packed_conv(parts, own, start, links, brick, scratch, pair_scratch, matrix, rim_matrix):
+    even, odd, edge, rims, down, up = scratch
+    next_even, next_odd, over = pair_scratch
+    held = []
+
+    def put(px, v):
+        even[px] = v.astype(BF16)
+        odd[px] = v[8:72].astype(BF16)
+        turned = pltpu.roll(v, 64, 1)
+        pairs = [(px - 1, merged(held[-1], turned))] if px else []
+        if px == SIDE + 1:
+            pairs.append((px, merged(v, jnp.zeros_like(v))))
+        for at, pair in pairs:
+            next_even[at] = pair.astype(BF16)
+            next_odd[at] = pair[8:72].astype(BF16)
+        if px >= 2:
+            over[px] = merged(v[0:64], turned[16:80]).astype(BF16)
+        held.append(v)
+
+    def put_rim(j, px, v):
+        edge[j, px] = v.astype(BF16)
+
+    fill(loader(parts, own), linker(links, brick, start, own, parts.shape[0]), put, rims, put_rim)
+    main, rim = stacked(even, odd, edge)
+    flat = lambda v: v.reshape(VOX, 128)
+    more = [next_even[0:8, 0:64], next_odd[0:8], next_even[0:8, 16:80], over[2:10], next_odd[2:10]]
+    sums = dot(jnp.concatenate([main] + [flat(v) for v in more], axis=1), matrix[...])
+    ends = jnp.concatenate([rim_matrix[:, 0:128], rim_matrix[:, 256:384]], axis=1)
+    edges = dot(rim, ends)
+    low_edge, high_edge = edges[:, 0:128], edges[:, 128:256]
+    low_edge = low_edge + pltpu.roll(low_edge, 64, 1)
+    high_edge = high_edge + pltpu.roll(high_edge, 64, 1)
+    front, back = sums[:, 0:128], sums[:, 128:256]
+    out = shifted_sum([front, pltpu.roll(front, 64, 1), back], jnp.concatenate([low_edge, high_edge], axis=1), down, up)
+    return out
 
 
 def coarse_conv(parts, own, start, links, brick, scratch, matrix):
@@ -405,6 +458,7 @@
     matrix, last_matrix, one_matrix, two_matrix,
     even, odd, edge, wide_even, wide_odd, wide_edge, rims, shift_down, shift_up,
     faces_even, faces_odd, face_edge, wide_faces_even, wide_faces_odd, wide_face_edge, wide_sums,
+    next_even, next_odd, over, tri_matrix, even_2, odd_2, edge_2, rims_2, down_2, up_2,
     parts, turned, hidden, halves, small, grown,
     x_send, x_halo, hidden_send, hidden_halo,
     code_block, codes, code_table, table, code_scalars, table_scalars,
@@ -618,6 +672,7 @@
     coarse_matrix(two_weight, two_matrix)
     fetches[4].wait()
     fine_matrix(out_weight, last_matrix)
+    packed_matrix(out_weight, tri_matrix)
     to_table.wait()
     to_codes.wait()
 
@@ -882,14 +937,21 @@
         unpack_pair(wire, halves, parts.at[at], parts.at[at + 1])
     out_both = two(out_bias)
 
-    def last_step(i, carry):
-        hidden[i] = fine_conv(parts, HALO + i, fine_start, fine_links, i, fine_scratch, last_matrix) + out_both
+    def last_step(pair, carry):
+        at = 2 * pair
+        first_sums, second_sums = (
+            packed_conv(
+                parts, HALO + at + one, fine_start, fine_links, at + one,
+                (even_2.at[one], odd_2.at[one], edge_2.at[one], rims_2.at[one], down_2.at[one], up_2.at[one]),
+                (next_even.at[one], next_odd.at[one], over.at[one]), tri_matrix, last_matrix,
+            )
+            for one in range(2)
+        )
+        flat = (merged(first_sums, pltpu.roll(second_sums, 64, 1)) + out_both).T
+        out[pl.ds(at, 2)] = x[pl.ds(at, 2)] + flat.reshape(2, 64, VOX)
         return carry
 
-    lax.fori_loop(0, count, last_step, 0)
-    for pair in range(pairs):
-        flat = merged(hidden[2 * pair], hidden[2 * pair + 1]).T
-        out[2 * pair : 2 * pair + 2] = x[2 * pair : 2 * pair + 2] + flat.reshape(2, 64, VOX)
+    lax.fori_loop(0, pairs, last_step, 0)
 
     end_halo_sends(x_copies)
     end_shared_sends(code_copies)
@@ -933,6 +995,9 @@
         halfs(1, 4, 2, 80, 128), halfs(1, 4, 2, 64, 128), halfs(1, 3, 2, 10, 16, 128),
         halfs(2, 4, slots, 80, 128), halfs(2, 4, slots, 64, 128), halfs(2, 3, slots, 10, 16, 128),
         floats(slots, VOX, 128),
+        halfs(2, 10, 80, 128), halfs(2, 10, 64, 128), halfs(2, 10, 64, 128), halfs(1792, 256),
+        halfs(2, 10, 80, 128), halfs(2, 10, 64, 128), halfs(2, 3, 10, 16, 128),
+        floats(2, 2, 10 * LINE, 128), floats(2, VOX + 16, 128), floats(2, VOX + 16, 128),
         floats(span, VOX, 128), floats(count // 2, VOX, 128), floats(count, VOX, 128),
         floats(2, SURFACE, 128), floats(128, 128), floats(HALO, VOX, 128),
         floats(2, SURFACE, 128), floats(2, SURFACE, 128), floats(2, SURFACE, 128), floats(2, SURFACE, 128),

time: 56.7 us -> 55.8 us (0.984)
  Pallas kernels: 54.5 us -> 53.7 us
    pallas_call x1, Pallas kernels: 54.5 us -> 53.7 us  [per_device(): pl.pallas_call(step_kernel, out_shape=jax.ShapeDtypeStruct(x.shape, F32),...]
where the time goes in v7:
time: 55.8 us; the launch traced here: 55.5 us
  Pallas kernels  53.7 us (96%)
  local copies, waits for them, and re-layouts  1.87 us (3%)
    pallas_call x1, Pallas kernels, per_device(): pl.pallas_call(step_kernel, out_shape=jax.ShapeDtypeStruct(x.shape, F32),...  53.7 us
    unnamed x1, local copies, waits for them, and re-layouts  1.87 us

profile of v7, /device:TPU:0, one launch (start us, length us, event | category | flops | bytes accessed | tf_op | source)
XLA Modules:
  0.0 55.5 jit_solution(2279208318430898786)
XLA Ops:
  0.0 53.7 %step.1 = f32[4,64,512]{2,1,0:T(8,128)} custom-call(f32[4,64,512]{2,1,0:T(8,128)} %x_any.1, s32[4,26]{1,0:T(4,128)} %fine_links.1, s32[4]{0:T(128)} %own_codes.1, s32[2,26]{1,0:T(2,128)} %coarse_links.1, f32[64,1728]{1,0:T(8,128)} %in_any.1, f32[1,64]{1,0:T(1,128)} %bitcast.6, f32[64,128]{1,0:T(8,128)} %bitcast.5, f32[128,3456]{1,0:T(8,128)} %one_any.1, ...), custom_call_target="tpu_custom_call" | custom-call | tf_op jit(solution)/shard_map/step/pallas_call | solution.py:1014
  53.7 1.9 %copy.16 = f32[4,64,512]{2,1,0:T(8,128)} copy(f32[4,64,512]{2,1,0:T(8,128)} %step.1) | data formatting | bytes 1048576
